TPU v7x, 32 devices: a whole 2x2x4 slice. The times are simulated.
32 devices in a mesh: ctx: 16 (over z, y, core), head: 2 (over x).
Axes of the slice: x: 2, y: 2, z: 4, core: 2. Of those that a mesh axis runs over, the one named last changes fastest.
Arguments:
- queries: bfloat16 [12288, 1024], P(('ctx', 'head')), may hold values from -64 to 64
- keys: bfloat16 [12288, 256], P(('ctx', 'head')), may hold values from -6 to 6
- values: bfloat16 [12288, 256], P(('ctx', 'head')), may hold values from -6 to 6
- out_grad: bfloat16 [12288, 1024], P(('ctx', 'head')), may hold values from -6 to 6
- rand_blocks: int32 [96, 3], replicated, may hold values from 0 to 95, as said below
- rand_count: int32 [96], replicated, may hold values from 1 to 3
Outputs:
- query_grad: bfloat16 [12288, 1024], P('ctx', 'head')
- key_grad: bfloat16 [12288, 256], P('ctx', 'head')
- value_grad: bfloat16 [12288, 256], P('ctx', 'head')
Inputs may be any that keep to these rules, and one draw needn't show every extreme that they name: Entry rand_blocks[b, r] names a block of a ctx shard (a range of 6 blocks) that is neither b's own shard nor either neighbour of it, counted modulo 16. The 18 entries of one shard's query blocks name blocks of one other shard at most 2 times, exactly 2 times for some shard.
All inputs are finite; a program needn't handle non-finite values.
Results may differ from a plain program's by a relative error of at most 0.0087.
Values may be sent and summed in bfloat16 or wider, within the bound.
A program may use at most 64 MiB of HBM per device.

v0:
```python
import math

import jax
import jax.numpy as jnp
from jax import lax
from jax.sharding import PartitionSpec as P

BLOCK = 128
HD = 128
GROUP = 4
G = 2
RAND = 3
QB_DEV = 6
NKB = 8


def broadcast(array, axis, root):
    mine = lax.axis_index(axis) == root
    return lax.psum(jnp.where(mine, array, jnp.zeros_like(array)), axis)


def attend(unused, inputs):
    query_tile, grad_tile, pair_tile, mask_row = inputs
    factor = 1.0 / math.sqrt(HD)
    key_tile = pair_tile[:, :, :HD].reshape(NKB * BLOCK, HD)
    value_tile = pair_tile[:, :, HD:].reshape(NKB * BLOCK, HD)
    key_mask = jnp.repeat(mask_row, BLOCK)
    scores = (
        jnp.einsum("tgh,kh->tgk", query_tile, key_tile, preferred_element_type=jnp.float32) * factor
    )
    scores = jnp.where(key_mask[None, None, :], scores, -jnp.inf)
    row_max = jnp.max(scores, axis=-1, keepdims=True)
    raw_weights = jnp.exp(scores - row_max)
    weights = raw_weights / jnp.sum(raw_weights, axis=-1, keepdims=True)
    weights_low = weights.astype(jnp.bfloat16)
    output = jnp.einsum("tgk,kh->tgh", weights_low, value_tile, preferred_element_type=jnp.float32)
    row_dot = jnp.sum(grad_tile.astype(jnp.float32) * output, axis=-1, keepdims=True)
    dprobs = jnp.einsum("tgh,kh->tgk", grad_tile, value_tile, preferred_element_type=jnp.float32)
    dscores = (weights * (dprobs - row_dot)).astype(jnp.bfloat16)
    dquery = (
        jnp.einsum("tgk,kh->tgh", dscores, key_tile, preferred_element_type=jnp.float32) * factor
    ).astype(jnp.bfloat16)
    key_part = (
        jnp.einsum("tgk,tgh->kh", dscores, query_tile, preferred_element_type=jnp.float32) * factor
    )
    value_part = jnp.einsum(
        "tgk,tgh->kh", weights_low, grad_tile, preferred_element_type=jnp.float32
    )
    pair_grad = jnp.concatenate(
        [key_part.reshape(NKB, BLOCK, HD), value_part.reshape(NKB, BLOCK, HD)], axis=-1
    )
    return (unused, (dquery, pair_grad))


def body(queries, keys, values, out_grad, rand_blocks, rand_count):
    head_queries, head_keys, head_values, head_grads = (
        lax.all_to_all(queries, "head", split_axis=1, concat_axis=0, tiled=True),
        lax.all_to_all(keys, "head", split_axis=1, concat_axis=0, tiled=True),
        lax.all_to_all(values, "head", split_axis=1, concat_axis=0, tiled=True),
        lax.all_to_all(out_grad, "head", split_axis=1, concat_axis=0, tiled=True),
    )
    shards = lax.axis_size("ctx")
    myself = lax.axis_index("ctx")
    per_dev = QB_DEV
    entries = per_dev * RAND
    owners_used = min(entries, shards - 3)
    capacity = (entries + owners_used - 1) // owners_used
    total_blocks = per_dev * shards
    far_slots = shards * capacity
    local_pairs = jnp.concatenate([head_keys, head_values], axis=1).reshape(per_dev, BLOCK, 2 * HD)
    global_pairs = broadcast(local_pairs[:G], "ctx", 0)
    flat_blocks = rand_blocks.reshape(shards, entries)
    owners = flat_blocks // per_dev
    offsets = flat_blocks % per_dev
    positions = jnp.arange(entries, dtype=jnp.int32)
    earlier = positions[None, :] < positions[:, None]
    same_owner = owners[:, :, None] == owners[:, None, :]
    slot_ranks = jnp.sum(same_owner & earlier[None], axis=2)
    slot_range = jnp.arange(capacity, dtype=jnp.int32)
    send_hits = (
        (owners == myself)[:, None, :] & (slot_ranks[:, None, :] == slot_range[None, :, None])
    ).astype(jnp.float32)
    offset_hot = (
        offsets[:, :, None] == jnp.arange(per_dev, dtype=jnp.int32)[None, None, :]
    ).astype(jnp.float32)
    send_table = jnp.einsum("dme,deq->dmq", send_hits, offset_hot)
    edge_base = per_dev + far_slots
    targets = jnp.arange(shards, dtype=jnp.int32)[:, None, None]
    first_slot = (slot_range == 0)[None, :, None]
    block_range = jnp.arange(per_dev, dtype=jnp.int32)[None, None, :]
    right_send = (targets == (myself + 1) % shards) & first_slot & (block_range == per_dev - 1)
    left_send = (targets == (myself - 1 + shards) % shards) & first_slot & (block_range == 0)
    send_table = send_table + right_send.astype(jnp.float32) + left_send.astype(jnp.float32)
    edge_pairs = jnp.zeros((0, BLOCK, 2 * HD), jnp.bfloat16)
    left_far = per_dev + (myself - 1 + shards) % shards * capacity
    right_far = per_dev + (myself + 1) % shards * capacity
    outgoing = jnp.einsum(
        "dmq,qtc->dmtc",
        send_table.astype(jnp.bfloat16),
        local_pairs,
        preferred_element_type=jnp.float32,
    ).astype(jnp.bfloat16)
    far_pairs = lax.all_to_all(outgoing, "ctx", split_axis=0, concat_axis=0, tiled=True)
    block_pool = jnp.concatenate(
        [local_pairs, far_pairs.reshape(far_slots, BLOCK, 2 * HD), edge_pairs, global_pairs], axis=0
    )
    local_index = jnp.arange(per_dev, dtype=jnp.int32)
    seq_block = myself * per_dev + local_index
    left_index = jnp.where(local_index > 0, local_index - 1, left_far)
    right_index = jnp.where(local_index < per_dev - 1, local_index + 1, right_far)
    global_index = jnp.broadcast_to(
        edge_base + jnp.arange(G, dtype=jnp.int32)[None, :], (per_dev, G)
    )
    my_owners = lax.dynamic_index_in_dim(owners, myself, 0, keepdims=False)
    my_ranks = lax.dynamic_index_in_dim(slot_ranks, myself, 0, keepdims=False)
    random_index = (per_dev + my_owners * capacity + my_ranks).reshape(per_dev, RAND)
    key_table = jnp.concatenate(
        [jnp.stack([left_index, local_index, right_index], axis=1), global_index, random_index],
        axis=1,
    )
    my_counts = lax.dynamic_slice_in_dim(rand_count, myself * per_dev, per_dev)
    key_valid = jnp.concatenate(
        [
            jnp.stack([seq_block > 0, seq_block >= 0, seq_block < total_blocks - 1], axis=1),
            jnp.ones((per_dev, G), bool),
            jnp.arange(RAND, dtype=jnp.int32)[None, :] < my_counts[:, None],
        ],
        axis=1,
    )
    remote = (key_table >= per_dev) & (key_table < edge_base)
    gathered = block_pool[key_table]
    query_tiles = head_queries.reshape(per_dev, BLOCK, GROUP, HD)
    grad_tiles = head_grads.reshape(per_dev, BLOCK, GROUP, HD)
    unused, (dq_tiles, pair_grads) = lax.scan(
        attend, jnp.zeros((), jnp.float32), (query_tiles, grad_tiles, gathered, key_valid)
    )
    lowered = lax.optimization_barrier(pair_grads.astype(jnp.bfloat16)).astype(jnp.float32)
    pair_grads = jnp.where(remote[:, :, None, None], lowered, pair_grads)
    pool_size = edge_base + G
    pool_hot = (
        key_table[:, :, None] == jnp.arange(pool_size, dtype=jnp.int32)[None, None, :]
    ).astype(jnp.float32)
    pool_grads = jnp.einsum("jnp,jntc->ptc", pool_hot, pair_grads, precision=lax.Precision.HIGHEST)
    local_grads = pool_grads[:per_dev]
    outgoing_grads = (
        pool_grads[per_dev:edge_base].reshape(shards, capacity, BLOCK, 2 * HD).astype(jnp.bfloat16)
    )
    returned = lax.all_to_all(outgoing_grads, "ctx", split_axis=0, concat_axis=0, tiled=True)
    local_grads = local_grads + jnp.einsum(
        "dmq,dmtc->qtc", send_table, returned.astype(jnp.float32), precision=lax.Precision.HIGHEST
    )
    global_total = lax.psum(pool_grads[edge_base:], "ctx")
    local_grads = local_grads.at[:G].add(
        jnp.where(myself == 0, global_total, jnp.zeros_like(global_total))
    )
    query_grad = dq_tiles.reshape(per_dev * BLOCK, GROUP * HD)
    key_grad = local_grads[:, :, :HD].reshape(per_dev * BLOCK, HD).astype(jnp.bfloat16)
    value_grad = local_grads[:, :, HD:].reshape(per_dev * BLOCK, HD).astype(jnp.bfloat16)
    return (query_grad, key_grad, value_grad)


def solution(mesh):
    placed = (
        P(("ctx", "head"), None),
        P(("ctx", "head"), None),
        P(("ctx", "head"), None),
        P(("ctx", "head"), None),
        P(),
        P(),
    )
    return jax.shard_map(
        body,
        mesh=mesh,
        in_specs=placed,
        out_specs=(P("ctx", "head"), P("ctx", "head"), P("ctx", "head")),
        check_vma=False,
    )
```

profile of v0, /device:TPU:0, one launch (start us, length us, event | category | flops | bytes accessed | tf_op | source)
XLA Modules:
  0.0 388.8 jit_solution(16370104756201506846)
XLA Ops:
  9.0 4.2 %all-to-all-start.2 = ((bf16[384,2,128]{0,2,1:T(8,128)(2,1)}), bf16[384,2,128]{0,2,1:T(8,128)(2,1)S(1)}, u32[]{:S(2)}, u32[]{:S(2)}) async-start(bf16[384,2,128]{0,2,1:T(8,128)(2,1)} %bitcast.24), calls=%async_computation.2 | async-start | bytes 393216 | tf_op jit(solution)/shard_map/all_to_all | solution.py:59
  14.6 2.1 copy.243
  19.0 3.5 all-to-all-start.1
  22.4 5.1 %all-to-all-done.1 = bf16[384,2,128]{0,2,1:T(8,128)(2,1)S(1)} async-done(((bf16[384,2,128]{0,2,1:T(8,128)(2,1)}), bf16[384,2,128]{0,2,1:T(8,128)(2,1)S(1)}, u32[]{:S(2)}, u32[]{:S(2)}) %all-to-all-start.1) | async-done | bytes 196640 | tf_op jit(solution)/shard_map/all_to_all | solution.py:58
  27.6 3.5 all-to-all-start
  32.7 8.9 %all-to-all-done = bf16[384,2,512]{2,0,1:T(8,128)(2,1)S(1)} async-done(((bf16[384,2,512]{2,0,1:T(8,128)(2,1)}), bf16[384,2,512]{2,0,1:T(8,128)(2,1)S(1)}, u32[]{:S(2)}, u32[]{:S(2)}) %all-to-all-start) | async-done | bytes 786464 | tf_op jit(solution)/shard_map/all_to_all | solution.py:57
  41.6 3.5 all-to-all-start.4
  46.2 2.1 copy.177
  48.3 6.4 %all-to-all-done.4 = bf16[384,2,512]{2,0,1:T(8,128)(2,1)S(1)} async-done(((bf16[384,2,512]{2,0,1:T(8,128)(2,1)}), bf16[384,2,512]{2,0,1:T(8,128)(2,1)S(1)}, u32[]{:S(2)}, u32[]{:S(2)}) %all-to-all-start.4) | async-done | bytes 786464 | tf_op jit(solution)/shard_map/all_to_all | solution.py:60
  55.7 5.1 %all-to-all-start.3 = ((bf16[16,2,128,256]{3,2,1,0:T(8,128)(2,1)}), bf16[16,2,128,256]{3,2,1,0:T(8,128)(2,1)S(1)}, u32[]{:S(2)}, u32[]{:S(2)}) async-start(bf16[16,2,128,256]{3,2,1,0:T(8,128)(2,1)} %copy.177), calls=%async_computation.3 | async-start | bytes 4194304 | tf_op jit(solution)/shard_map/all_to_all | solution.py:103
  68.1 104.0 %all-reduce.3.cloned.1.call-done = bf16[2,128,256]{2,1,0:T(8,128)(2,1)} async-done(((bf16[2,128,256]{2,1,0:T(8,128)(2,1)}), bf16[2,128,256]{2,1,0:T(8,128)(2,1)}) %all-reduce.3.cloned.1.call-update) | async-done | bytes 131088 | tf_op jit(solution)/shard_map/psum | solution.py:19
  175.5 2.6 gather_fusion
  178.1 49.3 %while.13 = (s32[]{:T(128)}, bf16[6,128,4,128]{3,2,1,0:T(4,128)(2,1)}, f32[6,8,128,256]{2,3,1,0:T(8,128)}, pred[6,8]{1,0:T(8,128)(4,1)S(1)}, bf16[6,128,4,128]{3...) while((s32[]{:T(128)}, ...), condition=%wide.region_6.7_spmd, body=%wide.region_2.6_spmd.sunk | while | flops 814414336 | bytes 22569096 | solution.py:134
  227.4 3.4 convert_element_type.57
  232.0 3.9 convert_select_fusion
  235.9 6.7 %copy.188 = f32[6,8,128,256]{3,1,0,2:T(8,128)} copy(f32[6,8,128,256]{2,3,1,0:T(8,128)} %convert_select_fusion) | data formatting | bytes 12582912 | tf_op jit(solution)/shard_map/jit(_where)/select_n | solution.py:138
  242.6 5.0 %convolution_bitcast_fusion.2 = f32[40,128,256]{2,0,1:T(8,128)S(1)} fusion(f32[6,8,128,256]{3,1,0,2:T(8,128)} %copy.188, s32[6,8]{1,0:T(8,128)S(1)} %concatenate.68), kind=kOutput, calls=%fused_computation.38 | convolution fusion | flops 754976640 | bytes 11534528 | tf_op jit(solution)/shard_map/jnp,jntc->ptc/dot_general | solution.py:143
  247.6 2.3 copy-done.1
  251.9 2.7 convert_element_type.59
  254.7 3.4 copy.189
  258.1 6.7 %all-to-all-start.5 = ((bf16[16,2,128,256]{3,1,2,0:T(2,128)(2,1)}), bf16[16,2,128,256]{3,1,2,0:T(2,128)(2,1)S(1)}, u32[]{:S(2)}, u32[]{:S(2)}) async-start(bf16[16,2,128,256]{3,1,2,0:T(2,128)(2,1)} %copy.189), calls=%async_computation.5 | async-start | bytes 4194304 | tf_op jit(solution)/shard_map/all_to_all | solution.py:148
  267.9 39.2 %all-to-all-done.5 = bf16[16,2,128,256]{3,1,2,0:T(2,128)(2,1)S(1)} async-done(((bf16[16,2,128,256]{3,1,2,0:T(2,128)(2,1)}), bf16[16,2,128,256]{3,1,2,0:T(2,128)(2,1)S(1)}, u32[]{:S(2)}, u32[]{:S(2)}) %all-to-all-start.5) | async-done | bytes 2097184 | tf_op jit(solution)/shard_map/all_to_all | solution.py:148
  307.1 3.2 fusion.24
  310.4 68.8 %all-reduce.5.cloned.1.call-done = f32[2,128,256]{2,0,1:T(2,128)} async-done(((f32[2,128,256]{2,0,1:T(2,128)}), f32[2,128,256]{2,0,1:T(2,128)}) %all-reduce.5.cloned.1.call-update) | async-done | bytes 262160 | tf_op jit(solution)/shard_map/psum | solution.py:152
  (181 shorter events, 77.6 us)
Async XLA Ops:
  7.2 9.6 %copy-start.8 = (bf16[384,256]{1,0:T(8,128)(2,1)S(1)}, bf16[384,256]{1,0:T(8,128)(2,1)}, u32[]{:S(2)}) copy-start(bf16[384,256]{1,0:T(8,128)(2,1)} %param.11) | copy-start | bytes 589828
  9.0 10.0 %all-to-all-start.2 = ((bf16[384,2,128]{0,2,1:T(8,128)(2,1)}), bf16[384,2,128]{0,2,1:T(8,128)(2,1)S(1)}, u32[]{:S(2)}, u32[]{:S(2)}) async-start(bf16[384,2,128]{0,2,1:T(8,128)(2,1)} %bitcast.24), calls=%async_computation.2 | async-start | bytes 393216 | tf_op jit(solution)/shard_map/all_to_all | solution.py:59
  14.6 16.7 %copy-start.6 = (bf16[384,1024]{1,0:T(8,128)(2,1)S(1)}, bf16[384,1024]{1,0:T(8,128)(2,1)}, u32[]{:S(2)}) copy-start(bf16[384,1024]{1,0:T(8,128)(2,1)} %param.13) | copy-start | bytes 2359300
  19.0 8.6 %all-to-all-start.1 = ((bf16[384,2,128]{0,2,1:T(8,128)(2,1)}), bf16[384,2,128]{0,2,1:T(8,128)(2,1)S(1)}, u32[]{:S(2)}, u32[]{:S(2)}) async-start(bf16[384,2,128]{0,2,1:T(8,128)(2,1)} %bitcast.21), calls=%async_computation.1 | async-start | bytes 393216 | tf_op jit(solution)/shard_map/all_to_all | solution.py:58
  27.6 14.0 %all-to-all-start = ((bf16[384,2,512]{2,0,1:T(8,128)(2,1)}), bf16[384,2,512]{2,0,1:T(8,128)(2,1)S(1)}, u32[]{:S(2)}, u32[]{:S(2)}) async-start(bf16[384,2,512]{2,0,1:T(8,128)(2,1)} %bitcast.127), calls=%async_computation | async-start | bytes 1572864 | tf_op jit(solution)/shard_map/all_to_all | solution.py:57
  32.4 13.8 %copy-start.4 = (bf16[2,384,128]{2,1,0:T(8,128)(2,1)}, bf16[2,384,128]{2,1,0:T(8,128)(2,1)S(1)}, u32[]{:S(2)}) copy-start(bf16[2,384,128]{2,1,0:T(8,128)(2,1)S(1)} %copy.168) | copy-start | bytes 589828
  32.6 9.0 %copy-start.5 = (bf16[2,384,128]{2,1,0:T(8,128)(2,1)}, bf16[2,384,128]{2,1,0:T(8,128)(2,1)S(1)}, u32[]{:S(2)}) copy-start(bf16[2,384,128]{2,1,0:T(8,128)(2,1)S(1)} %copy.166) | copy-start | bytes 589828
  41.6 13.1 %all-to-all-start.4 = ((bf16[384,2,512]{2,0,1:T(8,128)(2,1)}), bf16[384,2,512]{2,0,1:T(8,128)(2,1)S(1)}, u32[]{:S(2)}, u32[]{:S(2)}) async-start(bf16[384,2,512]{2,0,1:T(8,128)(2,1)} %bitcast.126), calls=%async_computation.4 | async-start | bytes 1572864 | tf_op jit(solution)/shard_map/all_to_all | solution.py:60
  48.3 14.2 %copy-start.9 = (s32[96]{0:T(128)S(1)}, s32[96]{0:T(128)}, u32[]{:S(2)}) copy-start(s32[96]{0:T(128)} %param.15) | copy-start | bytes 1156
  54.7 1.0 copy-start.3
  55.7 116.4 %all-to-all-start.3 = ((bf16[16,2,128,256]{3,2,1,0:T(8,128)(2,1)}), bf16[16,2,128,256]{3,2,1,0:T(8,128)(2,1)S(1)}, u32[]{:S(2)}, u32[]{:S(2)}) async-start(bf16[16,2,128,256]{3,2,1,0:T(8,128)(2,1)} %copy.177), calls=%async_computation.3 | async-start | bytes 4194304 | tf_op jit(solution)/shard_map/all_to_all | solution.py:103
  60.8 111.4 %all-reduce.3.cloned.1.call-start = ((), (), s32[]{:S(2)}) async-start(), calls=%async_computation.6 | async-start | bytes 262144 | tf_op jit(solution)/shard_map/psum | solution.py:19
  172.1 1.4 copy-start.2
  227.4 4.6 %copy-start = (f32[6,8,128,256]{2,3,1,0:T(8,128)S(1)}, f32[6,8,128,256]{2,3,1,0:T(8,128)}, u32[]{:S(2)}) copy-start(f32[6,8,128,256]{2,3,1,0:T(8,128)} %get-tuple-element.54) | copy-start | bytes 18874372
  247.6 2.3 copy-start.1
  258.1 8.8 %copy-start.7 = (bf16[6,128,4,128]{3,2,1,0:T(4,128)(2,1)S(1)}, bf16[6,128,4,128]{3,2,1,0:T(4,128)(2,1)}, u32[]{:S(2)}) copy-start(bf16[6,128,4,128]{3,2,1,0:T(4,128)(2,1)} %get-tuple-element.53) | copy-start | bytes 2359300
  258.1 49.1 %all-to-all-start.5 = ((bf16[16,2,128,256]{3,1,2,0:T(2,128)(2,1)}), bf16[16,2,128,256]{3,1,2,0:T(2,128)(2,1)S(1)}, u32[]{:S(2)}, u32[]{:S(2)}) async-start(bf16[16,2,128,256]{3,1,2,0:T(2,128)(2,1)} %copy.189), calls=%async_computation.5 | async-start | bytes 4194304 | tf_op jit(solution)/shard_map/all_to_all | solution.py:148
  264.8 114.4 %all-reduce.5.cloned.1.call-start = ((), (), s32[]{:S(2)}) async-start(), calls=%async_computation.7 | async-start | bytes 524288 | tf_op jit(solution)/shard_map/psum | solution.py:152
Sparse Core Ops, SparseCore 0:
  65.1 107.0 all-reduce.2
  269.0 110.0 all-reduce.4
where the time goes:
time: 390 us; the launch traced here: 389 us
  waiting for transfers between devices  232 us (59%)
  local copies, waits for them, and re-layouts  61.2 us (16%)
  matrix products  29.2 us (7%)
  starting transfers between devices  26.8 us (7%)
  other arithmetic  24.3 us (6%)
  between operations  14.4 us (4%)
    psum x1, waiting for transfers between devices, broadcast(): return lax.psum(jnp.where(mine, array, jnp.zeros_like(array)), axis)  104 us
    psum x1, waiting for transfers between devices, body(): global_total = lax.psum(pool_grads[edge_base:], 'ctx')  68.8 us
    all_to_all x1, waiting for transfers between devices, body(): lax.all_to_all(outgoing_grads, 'ctx', split_axis=0, concat_axis=0, tiled=...  39.2 us
    unnamed x24, local copies, waits for them, and re-layouts  9.57 us
    all_to_all x1, waiting for transfers between devices, body(): lax.all_to_all(queries, 'head', split_axis=1, concat_axis=0, tiled=True)  8.87 us
  transfers between devices with their start and end apart: 8, of which 6 were waited for; matrix products, arithmetic and copies ran while one was open for 6% of the time, Pallas kernels for 0%

commit v1 on v0

v1 whole, which is shorter than its diff:
```python
import math

import jax
import jax.numpy as jnp
from jax import lax
from jax.experimental import pallas as pl
from jax.experimental.pallas import tpu as pltpu
from jax.sharding import PartitionSpec as P

BLOCK = 128
HD = 128
GROUP = 4
G = 2
RAND = 3
QB_DEV = 6
NKB = 8
FACTOR = 1.0 / math.sqrt(HD)
EXP_FACTOR = FACTOR * math.log2(math.e)
CONTRACT_LAST = (((1,), (1,)), ((), ()))
CONTRACT_FIRST = (((0,), (0,)), ((), ()))
CONTRACT_MATMUL = (((1,), (0,)), ((), ()))


def dot(a, b, dims=CONTRACT_MATMUL):
    return lax.dot_general(a, b, dims, preferred_element_type=jnp.float32)


def attend_kernel(
    table, valid, query_ref, grad_ref, pool_ref,
    dquery_ref, local_ref, far_ref, total, scores, dprobs, dscores, keys,
):
    step = pl.program_id(0)
    per_dev = local_ref.shape[0]

    @pl.when(step == 0)
    def _():
        total[...] = jnp.zeros_like(total)

    query = jnp.concatenate([query_ref[:, h * HD : (h + 1) * HD] for h in range(GROUP)], axis=0)
    grad = jnp.concatenate([grad_ref[:, h * HD : (h + 1) * HD] for h in range(GROUP)], axis=0)
    rows = [slice(e * BLOCK, (e + 1) * BLOCK) for e in range(NKB)]
    entry = [table[step, e] for e in range(NKB)]
    row_max = None
    for e in range(NKB):
        key_tile = pool_ref[entry[e], :, :HD]
        keys[rows[e], :] = key_tile
        bias = jnp.where(valid[step, e] > 0, 0.0, -jnp.inf).astype(jnp.float32)
        tile = dot(key_tile, query, CONTRACT_LAST) + bias
        scores[rows[e], :] = tile
        tile_max = jnp.max(tile, axis=0, keepdims=True)
        row_max = tile_max if e == 0 else jnp.maximum(row_max, tile_max)
    row_sum = jnp.zeros_like(row_max)
    row_dot = jnp.zeros_like(row_max)
    for e in range(NKB):
        weight = jnp.exp2((scores[rows[e], :] - row_max) * EXP_FACTOR)
        dprob = dot(pool_ref[entry[e], :, HD:], grad, CONTRACT_LAST)
        row_sum += jnp.sum(weight, axis=0, keepdims=True)
        row_dot += jnp.sum(weight * dprob, axis=0, keepdims=True)
        scores[rows[e], :] = weight
        dprobs[rows[e], :] = dprob
    scale = 1.0 / row_sum
    row_dot = row_dot * scale
    for e in range(NKB):
        weight = scores[rows[e], :] * scale
        dscore = (weight * (dprobs[rows[e], :] - row_dot)).astype(jnp.bfloat16)
        dscores[rows[e], :] = dscore
        total[entry[e], :, :HD] += dot(dscore, query) * FACTOR
        total[entry[e], :, HD:] += dot(weight.astype(jnp.bfloat16), grad)
    dquery = dot(keys[...], dscores[...], CONTRACT_FIRST) * FACTOR
    for h in range(GROUP):
        dquery_ref[:, h * HD : (h + 1) * HD] = dquery[:, h * BLOCK : (h + 1) * BLOCK].T.astype(
            jnp.bfloat16
        )

    @pl.when(step == pl.num_programs(0) - 1)
    def _():
        local_ref[...] = total[:per_dev]
        far_ref[...] = total[per_dev:].astype(jnp.bfloat16)


def attend(table, valid, queries, grads, pool):
    pool_size = pool.shape[0]
    per_dev = table.shape[0]
    tile = pl.BlockSpec((BLOCK, GROUP * HD), lambda i, *_: (i, 0))
    whole = lambda size: pl.BlockSpec((size, BLOCK, 2 * HD), lambda i, *_: (0, 0, 0), pipeline_mode=pl.Buffered(1))
    return pl.pallas_call(
        attend_kernel,
        grid_spec=pltpu.PrefetchScalarGridSpec(
            num_scalar_prefetch=2,
            grid=(per_dev,),
            in_specs=[tile, tile, whole(pool_size)],
            out_specs=[tile, whole(per_dev), whole(pool_size - per_dev)],
            scratch_shapes=[
                pltpu.VMEM((pool_size, BLOCK, 2 * HD), jnp.float32),
                pltpu.VMEM((NKB * BLOCK, GROUP * BLOCK), jnp.float32),
                pltpu.VMEM((NKB * BLOCK, GROUP * BLOCK), jnp.float32),
                pltpu.VMEM((NKB * BLOCK, GROUP * BLOCK), jnp.bfloat16),
                pltpu.VMEM((NKB * BLOCK, HD), jnp.bfloat16),
            ],
        ),
        out_shape=[
            jax.ShapeDtypeStruct(queries.shape, jnp.bfloat16),
            jax.ShapeDtypeStruct((per_dev, BLOCK, 2 * HD), jnp.float32),
            jax.ShapeDtypeStruct((pool_size - per_dev, BLOCK, 2 * HD), jnp.bfloat16),
        ],
        compiler_params=pltpu.CompilerParams(vmem_limit_bytes=48 << 20),
        name="attend",
    )(table, valid, queries, grads, pool)


def exchange(array):
    return lax.all_to_all(array, "ctx", split_axis=0, concat_axis=0, tiled=True)


def body(queries, keys, values, out_grad, rand_blocks, rand_count):
    heads = lax.axis_size("head")
    shards = lax.axis_size("ctx")
    myself = lax.axis_index("ctx")
    per_dev = QB_DEV
    entries = per_dev * RAND
    owners_used = min(entries, shards - 3)
    capacity = (entries + owners_used - 1) // owners_used
    total_blocks = per_dev * shards
    far_slots = shards * capacity
    piece = G * BLOCK // shards

    tokens = keys.shape[0]
    pairs = jnp.stack([keys.reshape(tokens, heads, HD), values.reshape(tokens, heads, HD)], axis=2)
    pairs = pairs.transpose(1, 0, 2, 3).reshape(heads, tokens, 2 * HD)
    local_rows = lax.all_to_all(pairs, "head", split_axis=0, concat_axis=0, tiled=True)
    local_rows = local_rows.reshape(heads * tokens, 2 * HD)
    local_pairs = local_rows.reshape(per_dev, BLOCK, 2 * HD)
    head_queries = lax.all_to_all(queries, "head", split_axis=1, concat_axis=0, tiled=True)
    head_grads = lax.all_to_all(out_grad, "head", split_axis=1, concat_axis=0, tiled=True)

    flat_blocks = rand_blocks.reshape(shards, entries)
    owners = flat_blocks // per_dev
    offsets = flat_blocks % per_dev
    positions = jnp.arange(entries, dtype=jnp.int32)
    earlier = positions[None, :] < positions[:, None]
    same_owner = owners[:, :, None] == owners[:, None, :]
    slot_ranks = jnp.sum(same_owner & earlier[None], axis=2)
    slot_range = jnp.arange(capacity, dtype=jnp.int32)
    send_hits = (
        (owners == myself)[:, None, :] & (slot_ranks[:, None, :] == slot_range[None, :, None])
    ).astype(jnp.float32)
    offset_hot = (
        offsets[:, :, None] == jnp.arange(per_dev, dtype=jnp.int32)[None, None, :]
    ).astype(jnp.float32)
    send_table = jnp.einsum("dme,deq->dmq", send_hits, offset_hot)
    targets = jnp.arange(shards, dtype=jnp.int32)[:, None, None]
    first_slot = (slot_range == 0)[None, :, None]
    block_range = jnp.arange(per_dev, dtype=jnp.int32)[None, None, :]
    right_send = (targets == (myself + 1) % shards) & first_slot & (block_range == per_dev - 1)
    left_send = (targets == (myself - 1 + shards) % shards) & first_slot & (block_range == 0)
    send_table = send_table + right_send.astype(jnp.float32) + left_send.astype(jnp.float32)
    left_far = per_dev + (myself - 1 + shards) % shards * capacity
    right_far = per_dev + (myself + 1) % shards * capacity
    outgoing = jnp.einsum(
        "dmq,qtc->dmtc",
        send_table.astype(jnp.bfloat16),
        local_pairs,
        preferred_element_type=jnp.float32,
    ).astype(jnp.bfloat16)
    pieces = local_rows[: G * BLOCK].reshape(shards, piece, 2 * HD)
    packed = jnp.concatenate([outgoing.reshape(shards, capacity * BLOCK, 2 * HD), pieces], axis=1)
    arrived = exchange(packed)
    far_pairs = arrived[:, : capacity * BLOCK].reshape(far_slots, BLOCK, 2 * HD)
    my_piece = jnp.broadcast_to(arrived[0, capacity * BLOCK :][None], (shards, piece, 2 * HD))
    global_pairs = exchange(my_piece).reshape(G, BLOCK, 2 * HD)
    pool = jnp.concatenate([local_pairs, far_pairs, global_pairs], axis=0)

    edge_base = per_dev + far_slots
    local_index = jnp.arange(per_dev, dtype=jnp.int32)
    seq_block = myself * per_dev + local_index
    left_index = jnp.where(local_index > 0, local_index - 1, left_far)
    right_index = jnp.where(local_index < per_dev - 1, local_index + 1, right_far)
    global_index = jnp.broadcast_to(
        edge_base + jnp.arange(G, dtype=jnp.int32)[None, :], (per_dev, G)
    )
    my_owners = lax.dynamic_index_in_dim(owners, myself, 0, keepdims=False)
    my_ranks = lax.dynamic_index_in_dim(slot_ranks, myself, 0, keepdims=False)
    random_index = (per_dev + my_owners * capacity + my_ranks).reshape(per_dev, RAND)
    key_table = jnp.concatenate(
        [jnp.stack([left_index, local_index, right_index], axis=1), global_index, random_index],
        axis=1,
    ).astype(jnp.int32)
    my_counts = lax.dynamic_slice_in_dim(rand_count, myself * per_dev, per_dev)
    key_valid = jnp.concatenate(
        [
            jnp.stack([seq_block > 0, seq_block >= 0, seq_block < total_blocks - 1], axis=1),
            jnp.ones((per_dev, G), bool),
            jnp.arange(RAND, dtype=jnp.int32)[None, :] < my_counts[:, None],
        ],
        axis=1,
    ).astype(jnp.int32)

    query_grad, local_grads, far_grads = attend(key_table, key_valid, head_queries, head_grads, pool)

    packed_grads = jnp.concatenate(
        [
            far_grads[:far_slots].reshape(shards, capacity * BLOCK, 2 * HD),
            far_grads[far_slots:].reshape(shards, piece, 2 * HD),
        ],
        axis=1,
    )
    returned = exchange(packed_grads)
    returned_far = returned[:, : capacity * BLOCK].reshape(shards, capacity, BLOCK, 2 * HD)
    global_piece = jnp.sum(returned[:, capacity * BLOCK :].astype(jnp.float32), axis=0)
    global_piece = jnp.broadcast_to(global_piece[None].astype(jnp.bfloat16), (shards, piece, 2 * HD))
    global_total = exchange(global_piece).reshape(G, BLOCK, 2 * HD).astype(jnp.float32)
    local_grads = local_grads + jnp.einsum(
        "dmq,dmtc->qtc",
        send_table.astype(jnp.bfloat16),
        returned_far,
        preferred_element_type=jnp.float32,
    )
    local_grads = local_grads.at[:G].add(
        jnp.where(myself == 0, global_total, jnp.zeros_like(global_total))
    )
    key_grad = local_grads[:, :, :HD].reshape(per_dev * BLOCK, HD).astype(jnp.bfloat16)
    value_grad = local_grads[:, :, HD:].reshape(per_dev * BLOCK, HD).astype(jnp.bfloat16)
    return (query_grad, key_grad, value_grad)


def solution(mesh):
    placed = P(("ctx", "head"), None)
    return jax.shard_map(
        body,
        mesh=mesh,
        in_specs=(placed, placed, placed, placed, P(), P()),
        out_specs=(P("ctx", "head"), P("ctx", "head"), P("ctx", "head")),
        check_vma=False,
    )
```

time: 390 us -> 214 us (0.55)
  waiting for transfers between devices: 232 us -> 119 us
  local copies, waits for them, and re-layouts: 61.2 us -> 16.5 us
  matrix products: 29.2 us -> 2.32 us
  starting transfers between devices: 26.8 us -> 46.4 us
  Pallas kernels: 0 us -> 17.3 us
  other arithmetic: 24.3 us -> 10.6 us
  between operations: 14.4 us -> 1.01 us
    psum x2 -> x0, waiting for transfers between devices: 173 us -> none  [the longest x1 104 us: broadcast(): return lax.psum(jnp.where(mine, array, jnp.zeros_like(array)), axis)]
    all_to_all x4 -> x5, waiting for transfers between devices: 44.4 us -> 99.6 us  [the longest x4 94 us: exchange(): return lax.all_to_all(array, 'ctx', split_axis=0, concat_axis=0, tiled=True)]
    dot_general x38 -> x1, matrix products: 28.2 us -> 1.31 us  [body(): jnp.einsum('dmq,dmtc->qtc', send_table.astype(jnp.bfloat16), returned_far...]
    all_to_all x4 -> x5, starting transfers between devices: 19.4 us -> 39.3 us  [the longest x4 35.1 us: exchange(): return lax.all_to_all(array, 'ctx', split_axis=0, concat_axis=0, tiled=True)]
    pallas_call x0 -> x1, Pallas kernels: none -> 17.3 us  [attend(): pl.pallas_call(attend_kernel, grid_spec=pltpu.PrefetchScalarGridSpec(num_...]
    unnamed x24, local copies, waits for them, and re-layouts: 9.57 us -> 0.05 us
    convert_element_type x3 -> x0, local copies, waits for them, and re-layouts: 8.2 us -> none  [the longest x2 6.12 us: body(): pool_grads[per_dev:edge_base].reshape(shards, capacity, BLOCK, 2 * HD)]
    select_n x2 -> x0, local copies, waits for them, and re-layouts: 6.77 us -> none  [the longest x1 6.69 us: body(): pair_grads = jnp.where(remote[:, :, None, None], lowered, pair_grads)]
  transfers between devices with their start and end apart: 8 -> 7, of which waited for: 6 -> 7; matrix products, arithmetic and copies ran while one was open for 6% -> 6% of each run, Pallas kernels for 0% -> 0%
where the time goes in v1:
time: 214 us; the launch traced here: 213 us
  waiting for transfers between devices  119 us (56%)
  starting transfers between devices  46.4 us (22%)
  Pallas kernels  17.3 us (8%)
  local copies, waits for them, and re-layouts  16.5 us (8%)
  other arithmetic  10.6 us (5%)
  matrix products  2.32 us (1%)
    all_to_all x4, waiting for transfers between devices, exchange(): return lax.all_to_all(array, 'ctx', split_axis=0, concat_axis=0, tiled=True)  94 us
    all_to_all x4, starting transfers between devices, exchange(): return lax.all_to_all(array, 'ctx', split_axis=0, concat_axis=0, tiled=True)  35.1 us
    pallas_call x1, Pallas kernels, attend(): pl.pallas_call(attend_kernel, grid_spec=pltpu.PrefetchScalarGridSpec(num_...  17.3 us
    all_to_all x1, waiting for transfers between devices, body(): lax.all_to_all(queries, 'head', split_axis=1, concat_axis=0, tiled=True)  11.4 us
    all_to_all x1, waiting for transfers between devices, body(): lax.all_to_all(out_grad, 'head', split_axis=1, concat_axis=0, tiled=True)  7.6 us
    all_to_all x1, waiting for transfers between devices, body(): lax.all_to_all(pairs, 'head', split_axis=0, concat_axis=0, tiled=True)  5.63 us
  transfers between devices with their start and end apart: 7, of which 7 were waited for; matrix products, arithmetic and copies ran while one was open for 6% of the time, Pallas kernels for 0%

profile of v1, /device:TPU:0, one launch (start us, length us, event | category | flops | bytes accessed | tf_op | source)
XLA Modules:
  0.0 212.8 jit_solution(13015111873672003350)
XLA Ops:
  0.6 1.0 stack_reshape.6
  3.6 1.0 reshape.306
  4.6 4.2 %all-to-all-start.2 = ((bf16[2,384,256]{2,1,0:T(8,128)(2,1)}), bf16[2,384,256]{2,1,0:T(8,128)(2,1)S(1)}, u32[]{:S(2)}, u32[]{:S(2)}) async-start(bf16[2,384,256]{2,1,0:T(8,128)(2,1)} %reshape.306), calls=%async_computation.2 | async-start | bytes 786432 | tf_op jit(solution)/shard_map/all_to_all | solution.py:130
  10.5 5.6 %all-to-all-done.2 = bf16[2,384,256]{2,1,0:T(8,128)(2,1)S(1)} async-done(((bf16[2,384,256]{2,1,0:T(8,128)(2,1)}), bf16[2,384,256]{2,1,0:T(8,128)(2,1)S(1)}, u32[]{:S(2)}, u32[]{:S(2)}) %all-to-all-start.2) | async-done | bytes 393248 | tf_op jit(solution)/shard_map/all_to_all | solution.py:130
  17.7 1.5 pad_maximum_fusion.1
  19.3 6.3 %all-to-all-start.3 = ((bf16[16,272,256]{2,1,0:T(8,128)(2,1)}), bf16[16,272,256]{2,1,0:T(8,128)(2,1)S(1)}, u32[]{:S(2)}, u32[]{:S(2)}) async-start(bf16[16,272,256]{2,1,0:T(8,128)(2,1)} %pad_maximum_fusion.1), calls=%async_computation.3 | async-start | bytes 4456448 | tf_op jit(solution)/shard_map/all_to_all | solution.py:112
  26.5 42.4 %all-to-all-done.3 = bf16[16,272,256]{2,1,0:T(8,128)(2,1)S(1)} async-done(((bf16[16,272,256]{2,1,0:T(8,128)(2,1)}), bf16[16,272,256]{2,1,0:T(8,128)(2,1)S(1)}, u32[]{:S(2)}, u32[]{:S(2)}) %all-to-all-start.3) | async-done | bytes 2228256 | tf_op jit(solution)/shard_map/all_to_all | solution.py:112
  69.0 3.5 %all-to-all-start = ((bf16[384,2,512]{2,0,1:T(8,128)(2,1)}), bf16[384,2,512]{2,0,1:T(8,128)(2,1)S(1)}, u32[]{:S(2)}, u32[]{:S(2)}) async-start(bf16[384,2,512]{2,0,1:T(8,128)(2,1)} %bitcast.54), calls=%async_computation | async-start | bytes 1572864 | tf_op jit(solution)/shard_map/all_to_all | solution.py:133
  73.1 11.4 %all-to-all-done = bf16[384,2,512]{2,0,1:T(8,128)(2,1)S(1)} async-done(((bf16[384,2,512]{2,0,1:T(8,128)(2,1)}), bf16[384,2,512]{2,0,1:T(8,128)(2,1)S(1)}, u32[]{:S(2)}, u32[]{:S(2)}) %all-to-all-start) | async-done | bytes 786464 | tf_op jit(solution)/shard_map/all_to_all | solution.py:133
  85.2 11.3 %all-to-all-start.4 = ((bf16[16,16,256]{2,1,0:T(8,128)(2,1)}), bf16[16,16,256]{2,1,0:T(8,128)(2,1)S(1)}, u32[]{:S(2)}, u32[]{:S(2)}) async-start(bf16[16,16,256]{2,1,0:T(8,128)(2,1)} %broadcast_in_dim.21), calls=%async_computation.4 | async-start | bytes 262144 | tf_op jit(solution)/shard_map/all_to_all | solution.py:112
  99.0 1.4 concatenate.18
  101.8 2.1 copy.81
  104.4 3.5 %all-to-all-start.1 = ((bf16[384,2,512]{2,0,1:T(8,128)(2,1)}), bf16[384,2,512]{2,0,1:T(8,128)(2,1)S(1)}, u32[]{:S(2)}, u32[]{:S(2)}) async-start(bf16[384,2,512]{2,0,1:T(8,128)(2,1)} %bitcast.42), calls=%async_computation.1 | async-start | bytes 1572864 | tf_op jit(solution)/shard_map/all_to_all | solution.py:134
  108.1 1.6 slice-done
  109.7 1.8 pad_maximum_fusion.pool_ref
  111.5 7.6 %all-to-all-done.1 = bf16[384,2,512]{2,0,1:T(8,128)(2,1)S(1)} async-done(((bf16[384,2,512]{2,0,1:T(8,128)(2,1)}), bf16[384,2,512]{2,0,1:T(8,128)(2,1)S(1)}, u32[]{:S(2)}, u32[]{:S(2)}) %all-to-all-start.1) | async-done | bytes 786464 | tf_op jit(solution)/shard_map/all_to_all | solution.py:134
  119.1 17.3 %attend.1 = (bf16[768,512]{1,0:T(8,128)(2,1)}, f32[6,128,256]{2,1,0:T(8,128)S(1)}, bf16[34,128,256]{2,1,0:T(8,128)(2,1)S(1)}) custom-call(s32[6,8]{1,0:T(8,128)S(1)} %concatenate.17.table, s32[6,8]{1,0:T(8,128)S(1)} %convert_element_type.41.valid, bf16[768,512]{1,0:T(8,128)(2,1)S(1)} %bitcast.45, bf16[768,512]{1,0:T(8,128)(2,1)S(1)} %bitcast.46, ...), custom_call_target="tpu_custom_call" | custom-call | tf_op jit(solution)/shard_map/attend/pallas_call | solution.py:86
  136.7 1.5 pad_maximum_fusion.2
  138.2 5.8 %all-to-all-start.5 = ((bf16[16,272,256]{2,1,0:T(8,128)(2,1)}), bf16[16,272,256]{2,1,0:T(8,128)(2,1)}, u32[]{:S(2)}, u32[]{:S(2)}) async-start(bf16[16,272,256]{2,1,0:T(8,128)(2,1)} %pad_maximum_fusion.2), calls=%async_computation.5 | async-start | bytes 4456448 | tf_op jit(solution)/shard_map/all_to_all | solution.py:112
  144.0 43.4 %all-to-all-done.5 = bf16[16,272,256]{2,1,0:T(8,128)(2,1)} async-done(((bf16[16,272,256]{2,1,0:T(8,128)(2,1)}), bf16[16,272,256]{2,1,0:T(8,128)(2,1)}, u32[]{:S(2)}, u32[]{:S(2)}) %all-to-all-start.5) | async-done | bytes 2228256 | tf_op jit(solution)/shard_map/all_to_all | solution.py:112
  187.4 1.7 slice.66
  189.2 1.3 fusion.2
  192.1 11.7 %all-to-all-start.6 = ((bf16[16,16,256]{2,1,0:T(8,128)(2,1)}), bf16[16,16,256]{2,1,0:T(8,128)(2,1)S(1)}, u32[]{:S(2)}, u32[]{:S(2)}) async-start(bf16[16,16,256]{2,1,0:T(8,128)(2,1)} %broadcast_in_dim.22), calls=%async_computation.6 | async-start | bytes 262144 | tf_op jit(solution)/shard_map/all_to_all | solution.py:112
  204.2 7.6 %all-to-all-done.6 = bf16[16,16,256]{2,1,0:T(8,128)(2,1)S(1)} async-done(((bf16[16,16,256]{2,1,0:T(8,128)(2,1)}), bf16[16,16,256]{2,1,0:T(8,128)(2,1)S(1)}, u32[]{:S(2)}, u32[]{:S(2)}) %all-to-all-start.6) | async-done | bytes 131104 | tf_op jit(solution)/shard_map/all_to_all | solution.py:112
  (77 shorter events, 15.0 us)
Async XLA Ops:
  0.6 8.2 %copy-start.3 = (s32[96,3]{0,1:T(4,128)S(1)}, s32[96,3]{0,1:T(4,128)}, u32[]{:S(2)}) copy-start(s32[96,3]{0,1:T(4,128)} %param.12) | copy-start | bytes 3460
  4.6 11.5 %all-to-all-start.2 = ((bf16[2,384,256]{2,1,0:T(8,128)(2,1)}), bf16[2,384,256]{2,1,0:T(8,128)(2,1)S(1)}, u32[]{:S(2)}, u32[]{:S(2)}) async-start(bf16[2,384,256]{2,1,0:T(8,128)(2,1)} %reshape.306), calls=%async_computation.2 | async-start | bytes 786432 | tf_op jit(solution)/shard_map/all_to_all | solution.py:130
  8.8 8.9 %copy-start.8 = (pred[6]{0:T(512)(128)(4,1)}, pred[6]{0:T(512)(128)(4,1)S(1)}, u32[]{:S(2)}) copy-start(pred[6]{0:T(512)(128)(4,1)S(1)} %get-tuple-element.35) | copy-start | bytes 22
  8.8 8.9 %copy-start.10 = (pred[6]{0:T(512)(128)(4,1)}, pred[6]{0:T(512)(128)(4,1)S(1)}, u32[]{:S(2)}) copy-start(pred[6]{0:T(512)(128)(4,1)S(1)} %get-tuple-element.36) | copy-start | bytes 22
  10.1 7.6 %copy-start.2 = (s32[16,18]{1,0:T(8,128)}, s32[16,18]{1,0:T(8,128)S(1)}, u32[]{:S(2)}) copy-start(s32[16,18]{1,0:T(8,128)S(1)} %copy.56) | copy-start | bytes 3460
  10.5 7.3 %copy-start.4 = (pred[16,2]{0,1:T(4,128)(4,1)}, pred[16,2]{0,1:T(4,128)(4,1)S(1)}, u32[]{:S(2)}) copy-start(pred[16,2]{0,1:T(4,128)(4,1)S(1)} %get-tuple-element.27) | copy-start | bytes 100
  10.5 7.3 %copy-start.6 = (pred[16,2]{0,1:T(4,128)(4,1)}, pred[16,2]{0,1:T(4,128)(4,1)S(1)}, u32[]{:S(2)}) copy-start(pred[16,2]{0,1:T(4,128)(4,1)S(1)} %get-tuple-element.28) | copy-start | bytes 100
  19.3 6.3 %copy-start.1 = (bf16[384,1024]{1,0:T(8,128)(2,1)S(1)}, bf16[384,1024]{1,0:T(8,128)(2,1)}, u32[]{:S(2)}) copy-start(bf16[384,1024]{1,0:T(8,128)(2,1)} %param.8) | copy-start | bytes 2359300
  19.3 49.7 %all-to-all-start.3 = ((bf16[16,272,256]{2,1,0:T(8,128)(2,1)}), bf16[16,272,256]{2,1,0:T(8,128)(2,1)S(1)}, u32[]{:S(2)}, u32[]{:S(2)}) async-start(bf16[16,272,256]{2,1,0:T(8,128)(2,1)} %pad_maximum_fusion.1), calls=%async_computation.3 | async-start | bytes 4456448 | tf_op jit(solution)/shard_map/all_to_all | solution.py:112
  69.0 30.0 %copy-start = (bf16[16,272,256]{2,1,0:T(8,128)(2,1)}, bf16[16,272,256]{2,1,0:T(8,128)(2,1)S(1)}, u32[]{:S(2)}) copy-start(bf16[16,272,256]{2,1,0:T(8,128)(2,1)S(1)} %all-to-all-done.3) | copy-start | bytes 6684676
  69.0 15.5 %all-to-all-start = ((bf16[384,2,512]{2,0,1:T(8,128)(2,1)}), bf16[384,2,512]{2,0,1:T(8,128)(2,1)S(1)}, u32[]{:S(2)}, u32[]{:S(2)}) async-start(bf16[384,2,512]{2,0,1:T(8,128)(2,1)} %bitcast.54), calls=%async_computation | async-start | bytes 1572864 | tf_op jit(solution)/shard_map/all_to_all | solution.py:133
  85.2 19.2 %all-to-all-start.4 = ((bf16[16,16,256]{2,1,0:T(8,128)(2,1)}), bf16[16,16,256]{2,1,0:T(8,128)(2,1)S(1)}, u32[]{:S(2)}, u32[]{:S(2)}) async-start(bf16[16,16,256]{2,1,0:T(8,128)(2,1)} %broadcast_in_dim.21), calls=%async_computation.4 | async-start | bytes 262144 | tf_op jit(solution)/shard_map/all_to_all | solution.py:112
  104.4 14.7 %all-to-all-start.1 = ((bf16[384,2,512]{2,0,1:T(8,128)(2,1)}), bf16[384,2,512]{2,0,1:T(8,128)(2,1)S(1)}, u32[]{:S(2)}, u32[]{:S(2)}) async-start(bf16[384,2,512]{2,0,1:T(8,128)(2,1)} %bitcast.42), calls=%async_computation.1 | async-start | bytes 1572864 | tf_op jit(solution)/shard_map/all_to_all | solution.py:134
  108.1 1.6 slice-start
  138.2 49.3 %all-to-all-start.5 = ((bf16[16,272,256]{2,1,0:T(8,128)(2,1)}), bf16[16,272,256]{2,1,0:T(8,128)(2,1)}, u32[]{:S(2)}, u32[]{:S(2)}) async-start(bf16[16,272,256]{2,1,0:T(8,128)(2,1)} %pad_maximum_fusion.2), calls=%async_computation.5 | async-start | bytes 4456448 | tf_op jit(solution)/shard_map/all_to_all | solution.py:112
  144.0 45.2 %copy-start.5 = (pred[16,2]{0,1:T(4,128)(4,1)S(1)}, pred[16,2]{0,1:T(4,128)(4,1)}, u32[]{:S(2)}) copy-start(pred[16,2]{0,1:T(4,128)(4,1)} %copy-done.4) | copy-start | bytes 100
  144.0 45.2 %copy-start.7 = (pred[16,2]{0,1:T(4,128)(4,1)S(1)}, pred[16,2]{0,1:T(4,128)(4,1)}, u32[]{:S(2)}) copy-start(pred[16,2]{0,1:T(4,128)(4,1)} %copy-done.6) | copy-start | bytes 100
  144.0 45.2 %copy-start.9 = (pred[6]{0:T(512)(128)(4,1)S(1)}, pred[6]{0:T(512)(128)(4,1)}, u32[]{:S(2)}) copy-start(pred[6]{0:T(512)(128)(4,1)} %copy-done.8) | copy-start | bytes 22
  144.0 45.2 %copy-start.11 = (pred[6]{0:T(512)(128)(4,1)S(1)}, pred[6]{0:T(512)(128)(4,1)}, u32[]{:S(2)}) copy-start(pred[6]{0:T(512)(128)(4,1)} %copy-done.10) | copy-start | bytes 22
  192.1 19.7 %all-to-all-start.6 = ((bf16[16,16,256]{2,1,0:T(8,128)(2,1)}), bf16[16,16,256]{2,1,0:T(8,128)(2,1)S(1)}, u32[]{:S(2)}, u32[]{:S(2)}) async-start(bf16[16,16,256]{2,1,0:T(8,128)(2,1)} %broadcast_in_dim.22), calls=%async_computation.6 | async-start | bytes 262144 | tf_op jit(solution)/shard_map/all_to_all | solution.py:112

commit v2 on v1

--- a/solution.py
+++ b/solution.py
@@ -1,3 +1,4 @@
+import functools
 import math
 
 import jax
@@ -26,11 +27,23 @@
 
 
 def attend_kernel(
-    table, valid, query_ref, grad_ref, pool_ref,
+    direct, table, valid, query_ref, grad_ref, pool_ref,
     dquery_ref, local_ref, far_ref, total, scores, dprobs, dscores, keys,
 ):
     step = pl.program_id(0)
     per_dev = local_ref.shape[0]
+    first = 0
+    if direct:
+        first = lax.axis_index("ctx") * per_dev
+        block = first + step
+        last = pool_ref.shape[0] - 1
+        entry = [jnp.maximum(block - 1, 0), block, jnp.minimum(block + 1, last), 0, 1]
+        entry += [table[block, r] for r in range(RAND)]
+        use = [block > 0, True, block < last, True, True]
+        use += [r < valid[block] for r in range(RAND)]
+    else:
+        entry = [table[step, e] for e in range(NKB)]
+        use = [valid[step, e] > 0 for e in range(NKB)]
 
     @pl.when(step == 0)
     def _():
@@ -39,13 +52,13 @@
     query = jnp.concatenate([query_ref[:, h * HD : (h + 1) * HD] for h in range(GROUP)], axis=0)
     grad = jnp.concatenate([grad_ref[:, h * HD : (h + 1) * HD] for h in range(GROUP)], axis=0)
     rows = [slice(e * BLOCK, (e + 1) * BLOCK) for e in range(NKB)]
-    entry = [table[step, e] for e in range(NKB)]
     row_max = None
     for e in range(NKB):
         key_tile = pool_ref[entry[e], :, :HD]
         keys[rows[e], :] = key_tile
-        bias = jnp.where(valid[step, e] > 0, 0.0, -jnp.inf).astype(jnp.float32)
-        tile = dot(key_tile, query, CONTRACT_LAST) + bias
+        tile = dot(key_tile, query, CONTRACT_LAST)
+        if use[e] is not True:
+            tile += jnp.where(use[e], 0.0, -jnp.inf).astype(jnp.float32)
         scores[rows[e], :] = tile
         tile_max = jnp.max(tile, axis=0, keepdims=True)
         row_max = tile_max if e == 0 else jnp.maximum(row_max, tile_max)
@@ -74,22 +87,27 @@
 
     @pl.when(step == pl.num_programs(0) - 1)
     def _():
-        local_ref[...] = total[:per_dev]
-        far_ref[...] = total[per_dev:].astype(jnp.bfloat16)
-
-
-def attend(table, valid, queries, grads, pool):
+        local_ref[...] = total[pl.ds(first, per_dev)]
+        skip = total.shape[0] - far_ref.shape[0]
+
+        @pl.loop(0, far_ref.shape[0])
+        def _(i):
+            far_ref[i] = total[skip + i].astype(jnp.bfloat16)
+
+
+def attend(table, valid, queries, grads, pool, direct=False):
     pool_size = pool.shape[0]
-    per_dev = table.shape[0]
+    per_dev = QB_DEV
+    far_size = pool_size if direct else pool_size - per_dev
     tile = pl.BlockSpec((BLOCK, GROUP * HD), lambda i, *_: (i, 0))
     whole = lambda size: pl.BlockSpec((size, BLOCK, 2 * HD), lambda i, *_: (0, 0, 0), pipeline_mode=pl.Buffered(1))
     return pl.pallas_call(
-        attend_kernel,
+        functools.partial(attend_kernel, direct),
         grid_spec=pltpu.PrefetchScalarGridSpec(
             num_scalar_prefetch=2,
             grid=(per_dev,),
             in_specs=[tile, tile, whole(pool_size)],
-            out_specs=[tile, whole(per_dev), whole(pool_size - per_dev)],
+            out_specs=[tile, whole(per_dev), whole(far_size)],
             scratch_shapes=[
                 pltpu.VMEM((pool_size, BLOCK, 2 * HD), jnp.float32),
                 pltpu.VMEM((NKB * BLOCK, GROUP * BLOCK), jnp.float32),
@@ -101,7 +119,7 @@
         out_shape=[
             jax.ShapeDtypeStruct(queries.shape, jnp.bfloat16),
             jax.ShapeDtypeStruct((per_dev, BLOCK, 2 * HD), jnp.float32),
-            jax.ShapeDtypeStruct((pool_size - per_dev, BLOCK, 2 * HD), jnp.bfloat16),
+            jax.ShapeDtypeStruct((far_size, BLOCK, 2 * HD), jnp.bfloat16),
         ],
         compiler_params=pltpu.CompilerParams(vmem_limit_bytes=48 << 20),
         name="attend",
@@ -222,11 +240,376 @@
     value_grad = local_grads[:, :, HD:].reshape(per_dev * BLOCK, HD).astype(jnp.bfloat16)
     return (query_grad, key_grad, value_grad)
 
+MESH = pl.DeviceIdType.MESH
+LINE = 4
+SHARD = QB_DEV * BLOCK
+
+
+def place():
+    me = lax.axis_index("ctx")
+    return me // 4, (me // 2) % 2, me % 2
+
+
+def index_of(z, y, c):
+    return z * 4 + y * 2 + c
+
+
+def remote(src, dst, send_sem, recv_sem, **device):
+    return pltpu.make_async_remote_copy(
+        src_ref=src, dst_ref=dst, send_sem=send_sem, recv_sem=recv_sem, device_id=device, device_id_type=MESH
+    )
+
+
+def greet(z, y, c, head):
+    barrier = pltpu.get_barrier_semaphore()
+
+    def tell(**device):
+        pl.semaphore_signal(barrier, inc=1, device_id=device, device_id_type=MESH)
+
+    tell(ctx=index_of(z, 1 - y, c))
+    tell(ctx=index_of(z, y, 1 - c))
+    if head is not None:
+        tell(head=1 - head)
+
+    @pl.when(z > 0)
+    def _():
+        tell(ctx=index_of(z - 1, y, c))
+
+    @pl.when(z < LINE - 1)
+    def _():
+        tell(ctx=index_of(z + 1, y, c))
+
+    peers = (2 if head is None else 3) + (z + 2) // 3 + (5 - z) // 3
+    pl.semaphore_wait(barrier, peers)
+
+
+def gather_kernel(
+    q_in, k_in, v_in, g_in, q_out, g_out, pool,
+    local_sem, head_send, head_recv, up_send, down_send, y_send, c_send, z_recv, y_recv, c_recv,
+):
+    z, y, c = place()
+    me = index_of(z, y, c)
+    head = lax.axis_index("head")
+    other = 1 - head
+    tokens = k_in.shape[0]
+
+    def chunk(zz, yy, cc):
+        return pool.at[pl.ds(pl.multiple_of(index_of(zz, yy, cc) * SHARD, SHARD), SHARD), :]
+
+    pool_rows = pl.ds(pl.multiple_of(me * SHARD + head * tokens, tokens), tokens)
+    out_rows = pl.ds(pl.multiple_of(head * tokens, tokens), tokens)
+    jobs = []
+    for src, dst, width in (
+        (k_in, pool.at[pool_rows, :HD], HD),
+        (v_in, pool.at[pool_rows, HD:], HD),
+        (q_in, q_out.at[out_rows, :], GROUP * HD),
+        (g_in, g_out.at[out_rows, :], GROUP * HD),
+    ):
+        i = len(jobs)
+        mine = src.at[:, pl.ds(pl.multiple_of(head * width, width), width)]
+        theirs = src.at[:, pl.ds(pl.multiple_of(other * width, width), width)]
+        jobs.append(
+            (
+                pltpu.make_async_copy(mine, dst, local_sem.at[i]),
+                remote(theirs, dst, head_send.at[i], head_recv.at[i], head=other),
+            )
+        )
+    for local, _ in jobs:
+        local.start()
+    greet(z, y, c, head)
+    for _, away in jobs:
+        away.start()
+
+    def up(zz):
+        part = chunk(zz, y, c)
+        return remote(part, part, up_send.at[zz], z_recv.at[zz], ctx=index_of((z + 1) % LINE, y, c))
+
+    def down(zz):
+        part = chunk(zz, y, c)
+        return remote(part, part, down_send.at[zz], z_recv.at[zz], ctx=index_of((z + 3) % LINE, y, c))
+
+    def across(zz):
+        part = chunk(zz, y, c)
+        return remote(part, part, y_send.at[zz], y_recv.at[zz], ctx=index_of(z, 1 - y, c))
+
+    def beside(zz, yy):
+        part = chunk(zz, yy, c)
+        slot = zz * 2 + yy
+        return remote(part, part, c_send.at[slot], c_recv.at[slot], ctx=index_of(z, y, 1 - c))
+
+    for local, away in jobs[:2]:
+        local.wait()
+        away.wait_recv()
+
+    @pl.when(z < LINE - 1)
+    def _():
+        up(z).start()
+
+    @pl.when(z > 0)
+    def _():
+        down(z).start()
+
+    across(z).start()
+    beside(z, y).start()
+
+    def from_partner(zz):
+        across(zz).wait_recv()
+        beside(zz, 1 - y).start()
+
+    def stage(j, below, above):
+        @pl.when(z - j >= 0)
+        def _():
+            below(z - j)
+
+        @pl.when(z + j <= LINE - 1)
+        def _():
+            above(z + j)
+
+    def from_below(zz):
+        up(zz).wait_recv()
+
+        @pl.when(z < LINE - 1)
+        def _():
+            up(zz).start()
+
+        across(zz).start()
+        beside(zz, y).start()
+
+    def from_above(zz):
+        down(zz).wait_recv()
+
+        @pl.when(z > 0)
+        def _():
+            down(zz).start()
+
+        across(zz).start()
+        beside(zz, y).start()
+
+    for j in range(1, LINE):
+        stage(j, from_below, from_above)
+        if j == 1:
+            from_partner(z)
+        else:
+            stage(j - 1, from_partner, from_partner)
+    stage(LINE - 1, from_partner, from_partner)
+
+    for zz in range(LINE):
+        for yy in range(2):
+            beside(zz, yy).wait_recv()
+            beside(zz, yy).wait_send()
+        across(zz).wait_send()
+
+        @pl.when((z < LINE - 1) & (zz <= z))
+        def _():
+            up(zz).wait_send()
+
+        @pl.when((z > 0) & (zz >= z))
+        def _():
+            down(zz).wait_send()
+
+    for i, (local, away) in enumerate(jobs):
+        if i >= 2:
+            local.wait()
+            away.wait_recv()
+        away.wait_send()
+
+
+def gather(queries, keys, values, grads, total_blocks):
+    anywhere = pl.BlockSpec(memory_space=pl.ANY)
+    tokens = queries.shape[0]
+    moved = jax.ShapeDtypeStruct((2 * tokens, GROUP * HD), jnp.bfloat16)
+    dma = pltpu.SemaphoreType.DMA
+    return pl.pallas_call(
+        gather_kernel,
+        in_specs=[anywhere] * 4,
+        out_specs=[anywhere] * 3,
+        out_shape=[moved, moved, jax.ShapeDtypeStruct((total_blocks * BLOCK, 2 * HD), jnp.bfloat16)],
+        scratch_shapes=[
+            dma((4,)), dma((4,)), dma((4,)), dma((LINE,)), dma((LINE,)), dma((LINE,)), dma((2 * LINE,)),
+            dma((LINE,)), dma((LINE,)), dma((2 * LINE,)),
+        ],
+        compiler_params=pltpu.CompilerParams(collective_id=0, has_side_effects=True),
+        name="gather",
+    )(queries, keys, values, grads)
+
+
+def reduce_kernel(
+    grads, local, key_grad, value_grad,
+    c_in, y_out, y_in, z_out, z_in, total, c_send, c_recv, y_send, y_recv, z_send, z_recv,
+):
+    z, y, c = place()
+
+    def rows_of(zz, yy, cc):
+        return pl.multiple_of(index_of(zz, yy, cc) * SHARD, SHARD)
+
+    def beside(zz, yy):
+        slot = zz * 2 + yy
+        part = grads.at[pl.ds(rows_of(zz, yy, 1 - c), SHARD), :]
+        return remote(part, c_in.at[slot], c_send.at[slot], c_recv.at[slot], ctx=index_of(z, y, 1 - c))
+
+    def across(zz):
+        return remote(y_out.at[zz], y_in.at[zz], y_send.at[zz], y_recv.at[zz], ctx=index_of(z, 1 - y, c))
+
+    def up(zz):
+        return remote(z_out.at[zz], z_in.at[0, zz], z_send.at[zz], z_recv.at[0, zz], ctx=index_of((z + 1) % LINE, y, c))
+
+    def down(zz):
+        return remote(z_out.at[zz], z_in.at[1, zz], z_send.at[zz], z_recv.at[1, zz], ctx=index_of((z + 3) % LINE, y, c))
+
+    def pick(options):
+        return jnp.where(z == 0, options[0], jnp.where(z == 1, options[1], jnp.where(z == 2, options[2], options[3])))
+
+    order = [pick(options) for options in ((3, 3, 0, 0), (2, 0, 3, 1), (1, 2, 1, 2))] + [z]
+
+    greet(z, y, c, None)
+    for zz in order:
+        beside(zz, 1 - y).start()
+    for zz in order:
+        beside(zz, y).start()
+
+    def tiles(body):
+        @pl.loop(0, QB_DEV)
+        def _(i):
+            body(pl.multiple_of(i * BLOCK, BLOCK))
+
+    for zz in order:
+        beside(zz, 1 - y).wait_recv()
+        base = rows_of(zz, 1 - y, c)
+
+        def fold(row, zz=zz, base=base):
+            mine = grads[pl.ds(base + row, BLOCK), :].astype(jnp.float32)
+            theirs = c_in[zz * 2 + 1 - y, pl.ds(row, BLOCK), :].astype(jnp.float32)
+            y_out[zz, pl.ds(row, BLOCK), :] = (mine + theirs).astype(jnp.bfloat16)
+
+        tiles(fold)
+        across(zz).start()
+
+    for zz in order[:3]:
+        beside(zz, y).wait_recv()
+        across(zz).wait_recv()
+        base = rows_of(zz, y, c)
+
+        def gathered(row, zz=zz, base=base):
+            mine = grads[pl.ds(base + row, BLOCK), :].astype(jnp.float32)
+            theirs = c_in[zz * 2 + y, pl.ds(row, BLOCK), :].astype(jnp.float32)
+            return mine + theirs + y_in[zz, pl.ds(row, BLOCK), :].astype(jnp.float32)
+
+        def start(row):
+            z_out[zz, pl.ds(row, BLOCK), :] = gathered(row).astype(jnp.bfloat16)
+
+        def extend(side):
+            def body(row):
+                part = z_in[side, zz, pl.ds(row, BLOCK), :].astype(jnp.float32)
+                z_out[zz, pl.ds(row, BLOCK), :] = (gathered(row) + part).astype(jnp.bfloat16)
+
+            return body
+
+        @pl.when((z == 0) | (z == LINE - 1))
+        def _():
+            tiles(start)
+
+        @pl.when((z > 0) & (z < LINE - 1) & (zz > z))
+        def _():
+            up(zz).wait_recv()
+            tiles(extend(0))
+
+        @pl.when((z > 0) & (z < LINE - 1) & (zz < z))
+        def _():
+            down(zz).wait_recv()
+            tiles(extend(1))
+
+        @pl.when(zz > z)
+        def _():
+            up(zz).start()
+
+        @pl.when(zz < z)
+        def _():
+            down(zz).start()
+
+    beside(z, y).wait_recv()
+    across(z).wait_recv()
+
+    def own(row):
+        rows = pl.ds(row, BLOCK)
+        theirs = c_in[z * 2 + y, rows, :].astype(jnp.float32)
+        total[rows, :] = local[rows, :] + theirs + y_in[z, rows, :].astype(jnp.float32)
+
+    def add(side):
+        def body(row):
+            rows = pl.ds(row, BLOCK)
+            total[rows, :] += z_in[side, z, rows, :].astype(jnp.float32)
+
+        return body
+
+    tiles(own)
+
+    @pl.when(z > 0)
+    def _():
+        up(z).wait_recv()
+        tiles(add(0))
+
+    @pl.when(z < LINE - 1)
+    def _():
+        down(z).wait_recv()
+        tiles(add(1))
+
+    key_grad[...] = total[:, :HD].astype(jnp.bfloat16)
+    value_grad[...] = total[:, HD:].astype(jnp.bfloat16)
+
+    for zz in range(LINE):
+        beside(zz, 0).wait_send()
+        beside(zz, 1).wait_send()
+        across(zz).wait_send()
+
+        @pl.when(zz != z)
+        def _():
+            up(zz).wait_send()
+
+
+def reduce(grads, local):
+    in_vmem = pl.BlockSpec(memory_space=pltpu.VMEM)
+    dma = pltpu.SemaphoreType.DMA
+    part = (SHARD, 2 * HD)
+    result = jax.ShapeDtypeStruct((SHARD, HD), jnp.bfloat16)
+    return pl.pallas_call(
+        reduce_kernel,
+        in_specs=[in_vmem] * 2,
+        out_specs=[in_vmem] * 2,
+        out_shape=[result, result],
+        scratch_shapes=[
+            pltpu.VMEM((2 * LINE, *part), jnp.bfloat16),
+            pltpu.VMEM((LINE, *part), jnp.bfloat16),
+            pltpu.VMEM((LINE, *part), jnp.bfloat16),
+            pltpu.VMEM((LINE, *part), jnp.bfloat16),
+            pltpu.VMEM((2, LINE, *part), jnp.bfloat16),
+            pltpu.VMEM(part, jnp.float32),
+            dma((2 * LINE,)), dma((2 * LINE,)), dma((LINE,)), dma((LINE,)), dma((LINE,)), dma((2, LINE)),
+        ],
+        compiler_params=pltpu.CompilerParams(
+            collective_id=1, has_side_effects=True, vmem_limit_bytes=48 << 20
+        ),
+        name="reduce",
+    )(grads, local)
+
+
+def body_line(queries, keys, values, out_grad, rand_blocks, rand_count):
+    total_blocks = rand_blocks.shape[0]
+    head_queries, head_grads, pool = gather(queries, keys, values, out_grad, total_blocks)
+    pool = pool.reshape(total_blocks, BLOCK, 2 * HD)
+    query_grad, local_grads, all_grads = attend(
+        rand_blocks, rand_count, head_queries, head_grads, pool, direct=True
+    )
+    key_grad, value_grad = reduce(
+        all_grads.reshape(total_blocks * BLOCK, 2 * HD), local_grads.reshape(SHARD, 2 * HD)
+    )
+    return (query_grad, key_grad, value_grad)
+
 
 def solution(mesh):
+    line = mesh.shape["ctx"] == 4 * LINE and mesh.shape["head"] == 2
     placed = P(("ctx", "head"), None)
     return jax.shard_map(
-        body,
+        body_line if line else body,
         mesh=mesh,
         in_specs=(placed, placed, placed, placed, P(), P()),
         out_specs=(P("ctx", "head"), P("ctx", "head"), P("ctx", "head")),

time: 214 us -> 122 us (0.57)
  waiting for transfers between devices: 119 us -> 0 us
  Pallas kernels: 17.3 us -> 116 us
  starting transfers between devices: 46.4 us -> 0 us
  local copies, waits for them, and re-layouts: 16.5 us -> 5.05 us
  other arithmetic: 10.6 us -> 0 us
  matrix products: 2.32 us -> 0 us
    all_to_all x7 -> x0, waiting for transfers between devices: 119 us -> none  [the longest x4 94 us: exchange(): return lax.all_to_all(array, 'ctx', split_axis=0, concat_axis=0, tiled=True)]
    pallas_call x1 -> x3, Pallas kernels: 17.3 us -> 116 us  [the longest x1 47.4 us: gather(): pl.pallas_call(gather_kernel, in_specs=[anywhere] * 4, out_specs=[anywher...]
    all_to_all x7 -> x0, starting transfers between devices: 46.4 us -> none  [the longest x4 35.1 us: exchange(): return lax.all_to_all(array, 'ctx', split_axis=0, concat_axis=0, tiled=True)]
    unnamed x24 -> x9, local copies, waits for them, and re-layouts: 0.05 us -> 5.05 us
    concatenate x3 -> x0, other arithmetic: 4.89 us -> none  [the longest x1 1.84 us: body(): pool = jnp.concatenate([local_pairs, far_pairs, global_pairs], axis=0)]
    slice x7 -> x0, local copies, waits for them, and re-layouts: 4.39 us -> none  [the longest x1 1.73 us: body(): returned[:, :capacity * BLOCK].reshape(shards, capacity, BLOCK, 2 * HD)]
    all_to_all x2 -> x0, local copies, waits for them, and re-layouts: 3.01 us -> none  [the longest x1 2.07 us: body(): lax.all_to_all(out_grad, 'head', split_axis=1, concat_axis=0, tiled=True)]
    another operation x3 -> x0, local copies, waits for them, and re-layouts: 2.55 us -> none  [the longest x2 1.96 us: body(): jnp.stack([keys.reshape(tokens, heads, HD), values.reshape(tokens, heads,...]
  transfers between devices with their start and end apart: 7 -> 0, of which waited for: 7 -> 0; matrix products, arithmetic and copies ran while one was open for 6% -> 0% of each run, Pallas kernels for 0% -> 0%
where the time goes in v2:
time: 122 us
  Pallas kernels  116 us (95%)
  local copies, waits for them, and re-layouts  5.05 us (4%)
    pallas_call x1, Pallas kernels, gather(): pl.pallas_call(gather_kernel, in_specs=[anywhere] * 4, out_specs=[anywher...  47.4 us
    pallas_call x1, Pallas kernels, reduce(): pl.pallas_call(reduce_kernel, in_specs=[in_vmem] * 2, out_specs=[in_vmem]...  46.5 us
    pallas_call x1, Pallas kernels, attend(): pl.pallas_call(functools.partial(attend_kernel, direct), grid_spec=pltpu....  21.9 us
    unnamed x9, local copies, waits for them, and re-layouts  5.05 us

profile of v2, /device:TPU:0, one launch (start us, length us, event | category | flops | bytes accessed | tf_op | source)
XLA Modules:
  0.0 121.6 jit_solution(18172687731870339977)
XLA Ops:
  0.6 0.8 copy.9.table
  1.4 47.4 %gather.1 = (bf16[768,512]{1,0:T(8,128)(2,1)}, bf16[768,512]{1,0:T(8,128)(2,1)}, bf16[12288,256]{1,0:T(8,128)(2,1)}) custom-call(bf16[384,1024]{1,0:T(8,128)(2,1)} %q_in.1, bf16[384,256]{1,0:T(8,128)(2,1)} %k_in.1, bf16[384,256]{1,0:T(8,128)(2,1)} %v_in.1, bf16[384,1024]{1,0:T(8,128)(2,1)} %g_in.1), custom_call_target="tpu_custom_call" | custom-call | tf_op jit(solution)/shard_map/gather/pallas_call | solution.py:422
  48.8 0.0 copy-start
  48.9 1.1 copy-done
  50.0 0.0 copy-start.1
  50.0 1.1 copy-done.1
  51.1 0.0 copy-start.2
  51.1 0.7 copy-done.2
  51.8 21.9 %attend.1 = (bf16[768,512]{1,0:T(8,128)(2,1)}, f32[6,128,256]{2,1,0:T(8,128)S(1)}, bf16[96,128,256]{2,1,0:T(8,128)(2,1)}) custom-call(s32[96,3]{1,0:T(8,128)S(1)} %copy.9.table, s32[96]{0:T(128)S(1)} %copy-done.2, bf16[768,512]{1,0:T(8,128)(2,1)S(1)} %copy-done, bf16[768,512]{1,0:T(8,128)(2,1)S(1)} %copy-done.1, bf16[96,128,256]{2,1,0:T(8,128)(2,1)} %bitcast.5), custom_call_target="tpu_custom_call" | custom-call | tf_op jit(solution)/shard_map/attend/pallas_call | solution.py:104
  73.7 46.5 %reduce.1 = (bf16[768,128]{1,0:T(8,128)(2,1)S(1)}, bf16[768,128]{1,0:T(8,128)(2,1)S(1)}) custom-call(bf16[12288,256]{1,0:T(8,128)(2,1)} %bitcast.4, f32[768,256]{1,0:T(8,128)S(1)} %bitcast.3), custom_call_target="tpu_custom_call" | custom-call | tf_op jit(solution)/shard_map/reduce/pallas_call | solution.py:574
  120.2 0.7 copy.12
  120.9 0.7 copy.13
Async XLA Ops:
  48.8 1.1 copy-start
  50.0 1.1 copy-start.1
  51.1 0.7 copy-start.2

commit v3 on v2

--- a/solution.py
+++ b/solution.py
@@ -121,7 +121,7 @@
             jax.ShapeDtypeStruct((per_dev, BLOCK, 2 * HD), jnp.float32),
             jax.ShapeDtypeStruct((far_size, BLOCK, 2 * HD), jnp.bfloat16),
         ],
-        compiler_params=pltpu.CompilerParams(vmem_limit_bytes=48 << 20),
+        compiler_params=pltpu.CompilerParams(vmem_limit_bytes=62 << 20),
         name="attend",
     )(table, valid, queries, grads, pool)
 
@@ -293,8 +293,9 @@
     other = 1 - head
     tokens = k_in.shape[0]
 
-    def chunk(zz, yy, cc):
-        return pool.at[pl.ds(pl.multiple_of(index_of(zz, yy, cc) * SHARD, SHARD), SHARD), :]
+    def half(zz, yy, u):
+        start = index_of(zz, yy, c) * SHARD + u * tokens
+        return pool.at[pl.ds(pl.multiple_of(start, tokens), tokens), :]
 
     pool_rows = pl.ds(pl.multiple_of(me * SHARD + head * tokens, tokens), tokens)
     out_rows = pl.ds(pl.multiple_of(head * tokens, tokens), tokens)
@@ -317,95 +318,99 @@
     for local, _ in jobs:
         local.start()
     greet(z, y, c, head)
-    for _, away in jobs:
+    for _, away in jobs[:2]:
         away.start()
 
-    def up(zz):
-        part = chunk(zz, y, c)
-        return remote(part, part, up_send.at[zz], z_recv.at[zz], ctx=index_of((z + 1) % LINE, y, c))
-
-    def down(zz):
-        part = chunk(zz, y, c)
-        return remote(part, part, down_send.at[zz], z_recv.at[zz], ctx=index_of((z + 3) % LINE, y, c))
-
-    def across(zz):
-        part = chunk(zz, y, c)
-        return remote(part, part, y_send.at[zz], y_recv.at[zz], ctx=index_of(z, 1 - y, c))
-
-    def beside(zz, yy):
-        part = chunk(zz, yy, c)
-        slot = zz * 2 + yy
+    def up(zz, u):
+        part = half(zz, y, u)
+        slot = zz * 2 + u
+        return remote(part, part, up_send.at[slot], z_recv.at[slot], ctx=index_of((z + 1) % LINE, y, c))
+
+    def down(zz, u):
+        part = half(zz, y, u)
+        slot = zz * 2 + u
+        return remote(part, part, down_send.at[slot], z_recv.at[slot], ctx=index_of((z + 3) % LINE, y, c))
+
+    def across(zz, u):
+        part = half(zz, y, u)
+        slot = zz * 2 + u
+        return remote(part, part, y_send.at[slot], y_recv.at[slot], ctx=index_of(z, 1 - y, c))
+
+    def beside(zz, yy, u):
+        part = half(zz, yy, u)
+        slot = zz * 4 + yy * 2 + u
         return remote(part, part, c_send.at[slot], c_recv.at[slot], ctx=index_of(z, y, 1 - c))
 
-    for local, away in jobs[:2]:
+    def pass_on(zz, u, upward, downward):
+        if upward:
+
+            @pl.when(z < LINE - 1)
+            def _():
+                up(zz, u).start()
+
+        if downward:
+
+            @pl.when(z > 0)
+            def _():
+                down(zz, u).start()
+
+        across(zz, u).start()
+        beside(zz, y, u).start()
+
+    for local, _ in jobs[:2]:
         local.wait()
+    pass_on(z, head, True, True)
+    for _, away in jobs[:2]:
         away.wait_recv()
-
-    @pl.when(z < LINE - 1)
-    def _():
-        up(z).start()
-
-    @pl.when(z > 0)
-    def _():
-        down(z).start()
-
-    across(z).start()
-    beside(z, y).start()
-
-    def from_partner(zz):
-        across(zz).wait_recv()
-        beside(zz, 1 - y).start()
-
-    def stage(j, below, above):
+    pass_on(z, other, True, True)
+    for _, away in jobs[2:]:
+        away.start()
+
+    def from_partner(zz, u):
+        across(zz, u).wait_recv()
+        beside(zz, 1 - y, u).start()
+
+    def from_below(zz, u):
+        up(zz, u).wait_recv()
+        pass_on(zz, u, True, False)
+
+    def from_above(zz, u):
+        down(zz, u).wait_recv()
+        pass_on(zz, u, False, True)
+
+    def stage(j, u, below, above):
         @pl.when(z - j >= 0)
         def _():
-            below(z - j)
+            below(z - j, u)
 
         @pl.when(z + j <= LINE - 1)
         def _():
-            above(z + j)
-
-    def from_below(zz):
-        up(zz).wait_recv()
-
-        @pl.when(z < LINE - 1)
-        def _():
-            up(zz).start()
-
-        across(zz).start()
-        beside(zz, y).start()
-
-    def from_above(zz):
-        down(zz).wait_recv()
-
-        @pl.when(z > 0)
-        def _():
-            down(zz).start()
-
-        across(zz).start()
-        beside(zz, y).start()
+            above(z + j, u)
 
     for j in range(1, LINE):
-        stage(j, from_below, from_above)
-        if j == 1:
-            from_partner(z)
-        else:
-            stage(j - 1, from_partner, from_partner)
-    stage(LINE - 1, from_partner, from_partner)
+        for u in (head, other):
+            stage(j, u, from_below, from_above)
+            if j == 1:
+                from_partner(z, u)
+            else:
+                stage(j - 1, u, from_partner, from_partner)
+    for u in (head, other):
+        stage(LINE - 1, u, from_partner, from_partner)
 
     for zz in range(LINE):
-        for yy in range(2):
-            beside(zz, yy).wait_recv()
-            beside(zz, yy).wait_send()
-        across(zz).wait_send()
-
-        @pl.when((z < LINE - 1) & (zz <= z))
-        def _():
-            up(zz).wait_send()
-
-        @pl.when((z > 0) & (zz >= z))
-        def _():
-            down(zz).wait_send()
+        for u in range(2):
+            for yy in range(2):
+                beside(zz, yy, u).wait_recv()
+                beside(zz, yy, u).wait_send()
+            across(zz, u).wait_send()
+
+            @pl.when((z < LINE - 1) & (zz <= z))
+            def _():
+                up(zz, u).wait_send()
+
+            @pl.when((z > 0) & (zz >= z))
+            def _():
+                down(zz, u).wait_send()
 
     for i, (local, away) in enumerate(jobs):
         if i >= 2:
@@ -425,8 +430,8 @@
         out_specs=[anywhere] * 3,
         out_shape=[moved, moved, jax.ShapeDtypeStruct((total_blocks * BLOCK, 2 * HD), jnp.bfloat16)],
         scratch_shapes=[
-            dma((4,)), dma((4,)), dma((4,)), dma((LINE,)), dma((LINE,)), dma((LINE,)), dma((2 * LINE,)),
-            dma((LINE,)), dma((LINE,)), dma((2 * LINE,)),
+            dma((4,)), dma((4,)), dma((4,)), dma((2 * LINE,)), dma((2 * LINE,)), dma((2 * LINE,)), dma((4 * LINE,)),
+            dma((2 * LINE,)), dma((2 * LINE,)), dma((4 * LINE,)),
         ],
         compiler_params=pltpu.CompilerParams(collective_id=0, has_side_effects=True),
         name="gather",
@@ -435,141 +440,171 @@
 
 def reduce_kernel(
     grads, local, key_grad, value_grad,
-    c_in, y_out, y_in, z_out, z_in, total, c_send, c_recv, y_send, y_recv, z_send, z_recv,
+    c_in, y_out, y_in, z_out, z_in, c_send, c_recv, y_send, y_recv, z_send, z_recv,
 ):
     z, y, c = place()
 
-    def rows_of(zz, yy, cc):
-        return pl.multiple_of(index_of(zz, yy, cc) * SHARD, SHARD)
-
-    def beside(zz, yy):
-        slot = zz * 2 + yy
-        part = grads.at[pl.ds(rows_of(zz, yy, 1 - c), SHARD), :]
+    size = SHARD // 2
+
+    def rows_of(zz, yy, cc, u):
+        return pl.multiple_of(index_of(zz, yy, cc) * SHARD + u * size, size)
+
+    def beside(zz, yy, u):
+        slot = zz * 4 + yy * 2 + u
+        part = grads.at[pl.ds(rows_of(zz, yy, 1 - c, u), size), :]
         return remote(part, c_in.at[slot], c_send.at[slot], c_recv.at[slot], ctx=index_of(z, y, 1 - c))
 
-    def across(zz):
-        return remote(y_out.at[zz], y_in.at[zz], y_send.at[zz], y_recv.at[zz], ctx=index_of(z, 1 - y, c))
-
-    def up(zz):
-        return remote(z_out.at[zz], z_in.at[0, zz], z_send.at[zz], z_recv.at[0, zz], ctx=index_of((z + 1) % LINE, y, c))
-
-    def down(zz):
-        return remote(z_out.at[zz], z_in.at[1, zz], z_send.at[zz], z_recv.at[1, zz], ctx=index_of((z + 3) % LINE, y, c))
+    def across(zz, u):
+        slot = zz * 2 + u
+        return remote(
+            y_out.at[slot], y_in.at[slot], y_send.at[slot], y_recv.at[slot], ctx=index_of(z, 1 - y, c)
+        )
+
+    def up(zz, u):
+        slot = zz * 2 + u
+        return remote(
+            z_out.at[slot], z_in.at[0, slot], z_send.at[slot], z_recv.at[0, slot],
+            ctx=index_of((z + 1) % LINE, y, c),
+        )
+
+    def down(zz, u):
+        slot = zz * 2 + u
+        return remote(
+            z_out.at[slot], z_in.at[1, slot], z_send.at[slot], z_recv.at[1, slot],
+            ctx=index_of((z + 3) % LINE, y, c),
+        )
 
     def pick(options):
         return jnp.where(z == 0, options[0], jnp.where(z == 1, options[1], jnp.where(z == 2, options[2], options[3])))
 
     order = [pick(options) for options in ((3, 3, 0, 0), (2, 0, 3, 1), (1, 2, 1, 2))] + [z]
-
-    greet(z, y, c, None)
-    for zz in order:
-        beside(zz, 1 - y).start()
-    for zz in order:
-        beside(zz, y).start()
+    units = [(zz, u) for zz in order for u in range(2)]
+
+    def send_beside(i):
+        if i < len(units):
+            beside(units[i][0], 1 - y, units[i][1]).start()
+            beside(units[i][0], y, units[i][1]).start()
 
     def tiles(body):
-        @pl.loop(0, QB_DEV)
+        @pl.loop(0, size // BLOCK)
         def _(i):
             body(pl.multiple_of(i * BLOCK, BLOCK))
 
-    for zz in order:
-        beside(zz, 1 - y).wait_recv()
-        base = rows_of(zz, 1 - y, c)
-
-        def fold(row, zz=zz, base=base):
+    def fold_across(i):
+        zz, u = units[i]
+        beside(zz, 1 - y, u).wait_recv()
+        base = rows_of(zz, 1 - y, c, u)
+
+        def fold(row):
             mine = grads[pl.ds(base + row, BLOCK), :].astype(jnp.float32)
-            theirs = c_in[zz * 2 + 1 - y, pl.ds(row, BLOCK), :].astype(jnp.float32)
-            y_out[zz, pl.ds(row, BLOCK), :] = (mine + theirs).astype(jnp.bfloat16)
+            theirs = c_in[zz * 4 + (1 - y) * 2 + u, pl.ds(row, BLOCK), :].astype(jnp.float32)
+            y_out[zz * 2 + u, pl.ds(row, BLOCK), :] = (mine + theirs).astype(jnp.bfloat16)
 
         tiles(fold)
-        across(zz).start()
-
-    for zz in order[:3]:
-        beside(zz, y).wait_recv()
-        across(zz).wait_recv()
-        base = rows_of(zz, y, c)
-
-        def gathered(row, zz=zz, base=base):
-            mine = grads[pl.ds(base + row, BLOCK), :].astype(jnp.float32)
-            theirs = c_in[zz * 2 + y, pl.ds(row, BLOCK), :].astype(jnp.float32)
-            return mine + theirs + y_in[zz, pl.ds(row, BLOCK), :].astype(jnp.float32)
-
-        def start(row):
-            z_out[zz, pl.ds(row, BLOCK), :] = gathered(row).astype(jnp.bfloat16)
-
-        def extend(side):
+        if i >= 2:
+            across(*units[i - 2]).wait_send()
+        across(zz, u).start()
+
+    def along(i):
+        zz, u = units[i]
+        slot = zz * 2 + u
+        beside(zz, y, u).wait_recv()
+        across(zz, u).wait_recv()
+        base = rows_of(zz, y, c, u)
+
+        def gathered(row, mine):
+            theirs = c_in[zz * 4 + y * 2 + u, pl.ds(row, BLOCK), :].astype(jnp.float32)
+            return mine + theirs + y_in[slot, pl.ds(row, BLOCK), :].astype(jnp.float32)
+
+        def part(side, row):
+            return z_in[side, slot, pl.ds(row, BLOCK), :].astype(jnp.float32)
+
+        if i >= len(units) - 2:
+            own = pl.multiple_of(u * size, size)
+
+            def finish(*sides):
+                def body(row):
+                    rows = pl.ds(own + row, BLOCK)
+                    total = gathered(row, local[rows, :])
+                    for side in sides:
+                        total += part(side, row)
+                    key_grad[rows, :] = total[:, :HD].astype(jnp.bfloat16)
+                    value_grad[rows, :] = total[:, HD:].astype(jnp.bfloat16)
+
+                tiles(body)
+
+            @pl.when(z == 0)
+            def _():
+                down(zz, u).wait_recv()
+                finish(1)
+
+            @pl.when(z == LINE - 1)
+            def _():
+                up(zz, u).wait_recv()
+                finish(0)
+
+            @pl.when((z > 0) & (z < LINE - 1))
+            def _():
+                up(zz, u).wait_recv()
+                down(zz, u).wait_recv()
+                finish(0, 1)
+
+            return
+
+        def extend(*sides):
             def body(row):
-                part = z_in[side, zz, pl.ds(row, BLOCK), :].astype(jnp.float32)
-                z_out[zz, pl.ds(row, BLOCK), :] = (gathered(row) + part).astype(jnp.bfloat16)
-
-            return body
+                total = gathered(row, grads[pl.ds(base + row, BLOCK), :].astype(jnp.float32))
+                for side in sides:
+                    total += part(side, row)
+                z_out[slot, pl.ds(row, BLOCK), :] = total.astype(jnp.bfloat16)
+
+            tiles(body)
 
         @pl.when((z == 0) | (z == LINE - 1))
         def _():
-            tiles(start)
+            extend()
 
         @pl.when((z > 0) & (z < LINE - 1) & (zz > z))
         def _():
-            up(zz).wait_recv()
-            tiles(extend(0))
+            up(zz, u).wait_recv()
+            extend(0)
 
         @pl.when((z > 0) & (z < LINE - 1) & (zz < z))
         def _():
-            down(zz).wait_recv()
-            tiles(extend(1))
+            down(zz, u).wait_recv()
+            extend(1)
 
         @pl.when(zz > z)
         def _():
-            up(zz).start()
+            up(zz, u).start()
 
         @pl.when(zz < z)
         def _():
-            down(zz).start()
-
-    beside(z, y).wait_recv()
-    across(z).wait_recv()
-
-    def own(row):
-        rows = pl.ds(row, BLOCK)
-        theirs = c_in[z * 2 + y, rows, :].astype(jnp.float32)
-        total[rows, :] = local[rows, :] + theirs + y_in[z, rows, :].astype(jnp.float32)
-
-    def add(side):
-        def body(row):
-            rows = pl.ds(row, BLOCK)
-            total[rows, :] += z_in[side, z, rows, :].astype(jnp.float32)
-
-        return body
-
-    tiles(own)
-
-    @pl.when(z > 0)
-    def _():
-        up(z).wait_recv()
-        tiles(add(0))
-
-    @pl.when(z < LINE - 1)
-    def _():
-        down(z).wait_recv()
-        tiles(add(1))
-
-    key_grad[...] = total[:, :HD].astype(jnp.bfloat16)
-    value_grad[...] = total[:, HD:].astype(jnp.bfloat16)
-
-    for zz in range(LINE):
-        beside(zz, 0).wait_send()
-        beside(zz, 1).wait_send()
-        across(zz).wait_send()
-
-        @pl.when(zz != z)
-        def _():
-            up(zz).wait_send()
+            down(zz, u).start()
+
+    greet(z, y, c, None)
+    send_beside(0)
+    send_beside(1)
+    for i in range(len(units) + 2):
+        if i < len(units):
+            fold_across(i)
+            send_beside(i + 2)
+        if i >= 2:
+            along(i - 2)
+
+    for i, (zz, u) in enumerate(units):
+        beside(zz, 0, u).wait_send()
+        beside(zz, 1, u).wait_send()
+        if i >= len(units) - 2:
+            across(zz, u).wait_send()
+        else:
+            up(zz, u).wait_send()
 
 
 def reduce(grads, local):
     in_vmem = pl.BlockSpec(memory_space=pltpu.VMEM)
     dma = pltpu.SemaphoreType.DMA
-    part = (SHARD, 2 * HD)
+    part = (SHARD // 2, 2 * HD)
     result = jax.ShapeDtypeStruct((SHARD, HD), jnp.bfloat16)
     return pl.pallas_call(
         reduce_kernel,
@@ -577,13 +612,12 @@
         out_specs=[in_vmem] * 2,
         out_shape=[result, result],
         scratch_shapes=[
+            pltpu.VMEM((4 * LINE, *part), jnp.bfloat16),
             pltpu.VMEM((2 * LINE, *part), jnp.bfloat16),
-            pltpu.VMEM((LINE, *part), jnp.bfloat16),
-            pltpu.VMEM((LINE, *part), jnp.bfloat16),
-            pltpu.VMEM((LINE, *part), jnp.bfloat16),
-            pltpu.VMEM((2, LINE, *part), jnp.bfloat16),
-            pltpu.VMEM(part, jnp.float32),
-            dma((2 * LINE,)), dma((2 * LINE,)), dma((LINE,)), dma((LINE,)), dma((LINE,)), dma((2, LINE)),
+            pltpu.VMEM((2 * LINE, *part), jnp.bfloat16),
+            pltpu.VMEM((2 * LINE, *part), jnp.bfloat16),
+            pltpu.VMEM((2, 2 * LINE, *part), jnp.bfloat16),
+            dma((4 * LINE,)), dma((4 * LINE,)), dma((2 * LINE,)), dma((2 * LINE,)), dma((2 * LINE,)), dma((2, 2 * LINE)),
         ],
         compiler_params=pltpu.CompilerParams(
             collective_id=1, has_side_effects=True, vmem_limit_bytes=48 << 20

time: 122 us -> 116 us (0.951)
  Pallas kernels: 116 us -> 111 us
    pallas_call x1, Pallas kernels: 46.5 us -> 41.7 us  [reduce(): pl.pallas_call(reduce_kernel, in_specs=[in_vmem] * 2, out_specs=[in_vmem]...]
    unnamed x9 -> x5, local copies, waits for them, and re-layouts: 5.05 us -> 3.89 us
where the time goes in v3:
time: 116 us
  Pallas kernels  111 us (96%)
  local copies, waits for them, and re-layouts  3.89 us (3%)
    pallas_call x1, Pallas kernels, gather(): pl.pallas_call(gather_kernel, in_specs=[anywhere] * 4, out_specs=[anywher...  46.9 us
    pallas_call x1, Pallas kernels, reduce(): pl.pallas_call(reduce_kernel, in_specs=[in_vmem] * 2, out_specs=[in_vmem]...  41.7 us
    pallas_call x1, Pallas kernels, attend(): pl.pallas_call(functools.partial(attend_kernel, direct), grid_spec=pltpu....  22.6 us
    unnamed x5, local copies, waits for them, and re-layouts  3.89 us

profile of v3, /device:TPU:0, one launch (start us, length us, event | category | flops | bytes accessed | tf_op | source)
XLA Modules:
  0.0 115.7 jit_solution(8544583982694404207)
XLA Ops:
  0.6 1.4 %copy.9.table = s32[96,3]{1,0:T(8,128)} copy(s32[96,3]{0,1:T(4,128)} %param.10) | data formatting | bytes 2304 | tf_op args[4]
  2.0 46.9 %gather.1 = (bf16[768,512]{1,0:T(8,128)(2,1)}, bf16[768,512]{1,0:T(8,128)(2,1)}, bf16[12288,256]{1,0:T(8,128)(2,1)}) custom-call(bf16[384,1024]{1,0:T(8,128)(2,1)} %q_in.1, bf16[384,256]{1,0:T(8,128)(2,1)} %k_in.1, bf16[384,256]{1,0:T(8,128)(2,1)} %v_in.1, bf16[384,1024]{1,0:T(8,128)(2,1)} %g_in.1), custom_call_target="tpu_custom_call" | custom-call | tf_op jit(solution)/shard_map/gather/pallas_call | solution.py:427
  49.0 22.6 %attend.1 = (bf16[768,512]{1,0:T(8,128)(2,1)}, f32[6,128,256]{2,1,0:T(8,128)}, bf16[96,128,256]{2,1,0:T(8,128)(2,1)}) custom-call(s32[96,3]{1,0:T(8,128)} %copy.9.table, s32[96]{0:T(128)} %valid.1, bf16[768,512]{1,0:T(8,128)(2,1)} %get-tuple-element.11.query_ref, bf16[768,512]{1,0:T(8,128)(2,1)} %get-tuple-element.12.grad_ref, bf16[96,128,256]{2,1,0:T(8,128)(2,1)} %bitcast.5), custom_call_target="tpu_custom_call" | custom-call | tf_op jit(solution)/shard_map/attend/pallas_call | solution.py:104
  71.5 0.0 copy-start
  71.5 1.1 copy-done
  72.7 41.7 %reduce.1 = (bf16[768,128]{1,0:T(8,128)(2,1)S(1)}, bf16[768,128]{1,0:T(8,128)(2,1)S(1)}) custom-call(bf16[12288,256]{1,0:T(8,128)(2,1)} %bitcast.4, f32[768,256]{1,0:T(8,128)S(1)} %bitcast.3), custom_call_target="tpu_custom_call" | custom-call | tf_op jit(solution)/shard_map/reduce/pallas_call | solution.py:609
  114.4 0.7 copy.12
  115.1 0.7 copy.13
Async XLA Ops:
  71.5 1.1 copy-start

commit v4 on v3

--- a/solution.py
+++ b/solution.py
@@ -27,8 +27,8 @@
 
 
 def attend_kernel(
-    direct, table, valid, query_ref, grad_ref, pool_ref,
-    dquery_ref, local_ref, far_ref, total, scores, dprobs, dscores, keys,
+    direct, table, valid, query_ref, grad_ref, pool_hbm,
+    dquery_ref, local_ref, far_ref, total, scores, dprobs, dscores, keys, held, sems,
 ):
     step = pl.program_id(0)
     per_dev = local_ref.shape[0]
@@ -36,9 +36,9 @@
     if direct:
         first = lax.axis_index("ctx") * per_dev
         block = first + step
-        last = pool_ref.shape[0] - 1
+        last = held.shape[0] - 1
         entry = [jnp.maximum(block - 1, 0), block, jnp.minimum(block + 1, last), 0, 1]
-        entry += [table[block, r] for r in range(RAND)]
+        entry += [table[r, block] for r in range(RAND)]
         use = [block > 0, True, block < last, True, True]
         use += [r < valid[block] for r in range(RAND)]
     else:
@@ -47,14 +47,17 @@
 
     @pl.when(step == 0)
     def _():
+        load = pltpu.make_async_copy(pool_hbm, held, sems.at[0])
+        load.start()
         total[...] = jnp.zeros_like(total)
+        load.wait()
 
     query = jnp.concatenate([query_ref[:, h * HD : (h + 1) * HD] for h in range(GROUP)], axis=0)
     grad = jnp.concatenate([grad_ref[:, h * HD : (h + 1) * HD] for h in range(GROUP)], axis=0)
     rows = [slice(e * BLOCK, (e + 1) * BLOCK) for e in range(NKB)]
     row_max = None
     for e in range(NKB):
-        key_tile = pool_ref[entry[e], :, :HD]
+        key_tile = held[entry[e], :, :HD]
         keys[rows[e], :] = key_tile
         tile = dot(key_tile, query, CONTRACT_LAST)
         if use[e] is not True:
@@ -66,7 +69,7 @@
     row_dot = jnp.zeros_like(row_max)
     for e in range(NKB):
         weight = jnp.exp2((scores[rows[e], :] - row_max) * EXP_FACTOR)
-        dprob = dot(pool_ref[entry[e], :, HD:], grad, CONTRACT_LAST)
+        dprob = dot(held[entry[e], :, HD:], grad, CONTRACT_LAST)
         row_sum += jnp.sum(weight, axis=0, keepdims=True)
         row_dot += jnp.sum(weight * dprob, axis=0, keepdims=True)
         scores[rows[e], :] = weight
@@ -92,13 +95,17 @@
 
         @pl.loop(0, far_ref.shape[0])
         def _(i):
-            far_ref[i] = total[skip + i].astype(jnp.bfloat16)
+            held[i] = total[skip + i].astype(jnp.bfloat16)
+            pltpu.make_async_copy(held.at[i], far_ref.at[i], sems.at[1]).start()
+
+        pltpu.make_async_copy(held.at[pl.ds(0, far_ref.shape[0])], far_ref, sems.at[1]).wait()
 
 
 def attend(table, valid, queries, grads, pool, direct=False):
     pool_size = pool.shape[0]
     per_dev = QB_DEV
     far_size = pool_size if direct else pool_size - per_dev
+    anywhere = pl.BlockSpec(memory_space=pl.ANY)
     tile = pl.BlockSpec((BLOCK, GROUP * HD), lambda i, *_: (i, 0))
     whole = lambda size: pl.BlockSpec((size, BLOCK, 2 * HD), lambda i, *_: (0, 0, 0), pipeline_mode=pl.Buffered(1))
     return pl.pallas_call(
@@ -106,14 +113,16 @@
         grid_spec=pltpu.PrefetchScalarGridSpec(
             num_scalar_prefetch=2,
             grid=(per_dev,),
-            in_specs=[tile, tile, whole(pool_size)],
-            out_specs=[tile, whole(per_dev), whole(far_size)],
+            in_specs=[tile, tile, anywhere],
+            out_specs=[tile, whole(per_dev), anywhere],
             scratch_shapes=[
                 pltpu.VMEM((pool_size, BLOCK, 2 * HD), jnp.float32),
                 pltpu.VMEM((NKB * BLOCK, GROUP * BLOCK), jnp.float32),
                 pltpu.VMEM((NKB * BLOCK, GROUP * BLOCK), jnp.float32),
                 pltpu.VMEM((NKB * BLOCK, GROUP * BLOCK), jnp.bfloat16),
                 pltpu.VMEM((NKB * BLOCK, HD), jnp.bfloat16),
+                pltpu.VMEM((pool_size, BLOCK, 2 * HD), jnp.bfloat16),
+                pltpu.SemaphoreType.DMA((2,)),
             ],
         ),
         out_shape=[
@@ -439,11 +448,10 @@
 
 
 def reduce_kernel(
-    grads, local, key_grad, value_grad,
-    c_in, y_out, y_in, z_out, z_in, c_send, c_recv, y_send, y_recv, z_send, z_recv,
+    grads, local_hbm, key_grad, value_grad,
+    held, local, c_in, y_out, y_in, z_out, z_in, h_sem, c_send, c_recv, y_send, y_recv, z_send, z_recv,
 ):
     z, y, c = place()
-
     size = SHARD // 2
 
     def rows_of(zz, yy, cc, u):
@@ -485,6 +493,12 @@
             beside(units[i][0], 1 - y, units[i][1]).start()
             beside(units[i][0], y, units[i][1]).start()
 
+    def hold(zz, yy):
+        part = grads.at[pl.ds(rows_of(zz, yy, c, 0), SHARD), :]
+        return pltpu.make_async_copy(part, held.at[zz * 2 + yy], h_sem.at[zz * 2 + yy])
+
+    hold_local = pltpu.make_async_copy(local_hbm, local, h_sem.at[2 * LINE])
+
     def tiles(body):
         @pl.loop(0, size // BLOCK)
         def _(i):
@@ -492,11 +506,12 @@
 
     def fold_across(i):
         zz, u = units[i]
+        if u == 0:
+            hold(zz, 1 - y).wait()
         beside(zz, 1 - y, u).wait_recv()
-        base = rows_of(zz, 1 - y, c, u)
 
         def fold(row):
-            mine = grads[pl.ds(base + row, BLOCK), :].astype(jnp.float32)
+            mine = held[zz * 2 + 1 - y, pl.ds(u * size + row, BLOCK), :].astype(jnp.float32)
             theirs = c_in[zz * 4 + (1 - y) * 2 + u, pl.ds(row, BLOCK), :].astype(jnp.float32)
             y_out[zz * 2 + u, pl.ds(row, BLOCK), :] = (mine + theirs).astype(jnp.bfloat16)
 
@@ -508,9 +523,10 @@
     def along(i):
         zz, u = units[i]
         slot = zz * 2 + u
+        if u == 0:
+            hold(zz, y).wait()
         beside(zz, y, u).wait_recv()
         across(zz, u).wait_recv()
-        base = rows_of(zz, y, c, u)
 
         def gathered(row, mine):
             theirs = c_in[zz * 4 + y * 2 + u, pl.ds(row, BLOCK), :].astype(jnp.float32)
@@ -520,11 +536,13 @@
             return z_in[side, slot, pl.ds(row, BLOCK), :].astype(jnp.float32)
 
         if i >= len(units) - 2:
-            own = pl.multiple_of(u * size, size)
+            own = u * size
+            if u == 0:
+                hold_local.wait()
 
             def finish(*sides):
                 def body(row):
-                    rows = pl.ds(own + row, BLOCK)
+                    rows = pl.ds(pl.multiple_of(own + row, BLOCK), BLOCK)
                     total = gathered(row, local[rows, :])
                     for side in sides:
                         total += part(side, row)
@@ -553,7 +571,7 @@
 
         def extend(*sides):
             def body(row):
-                total = gathered(row, grads[pl.ds(base + row, BLOCK), :].astype(jnp.float32))
+                total = gathered(row, held[zz * 2 + y, pl.ds(u * size + row, BLOCK), :].astype(jnp.float32))
                 for side in sides:
                     total += part(side, row)
                 z_out[slot, pl.ds(row, BLOCK), :] = total.astype(jnp.bfloat16)
@@ -582,6 +600,10 @@
         def _():
             down(zz, u).start()
 
+    for zz in order:
+        hold(zz, 1 - y).start()
+        hold(zz, y).start()
+    hold_local.start()
     greet(z, y, c, None)
     send_beside(0)
     send_beside(1)
@@ -608,19 +630,21 @@
     result = jax.ShapeDtypeStruct((SHARD, HD), jnp.bfloat16)
     return pl.pallas_call(
         reduce_kernel,
-        in_specs=[in_vmem] * 2,
+        in_specs=[pl.BlockSpec(memory_space=pl.ANY)] * 2,
         out_specs=[in_vmem] * 2,
         out_shape=[result, result],
         scratch_shapes=[
+            pltpu.VMEM((2 * LINE, SHARD, 2 * HD), jnp.bfloat16),
+            pltpu.VMEM((SHARD, 2 * HD), jnp.float32),
             pltpu.VMEM((4 * LINE, *part), jnp.bfloat16),
             pltpu.VMEM((2 * LINE, *part), jnp.bfloat16),
             pltpu.VMEM((2 * LINE, *part), jnp.bfloat16),
             pltpu.VMEM((2 * LINE, *part), jnp.bfloat16),
             pltpu.VMEM((2, 2 * LINE, *part), jnp.bfloat16),
-            dma((4 * LINE,)), dma((4 * LINE,)), dma((2 * LINE,)), dma((2 * LINE,)), dma((2 * LINE,)), dma((2, 2 * LINE)),
+            dma((2 * LINE + 1,)), dma((4 * LINE,)), dma((4 * LINE,)), dma((2 * LINE,)), dma((2 * LINE,)), dma((2 * LINE,)), dma((2, 2 * LINE)),
         ],
         compiler_params=pltpu.CompilerParams(
-            collective_id=1, has_side_effects=True, vmem_limit_bytes=48 << 20
+            collective_id=1, has_side_effects=True, vmem_limit_bytes=62 << 20
         ),
         name="reduce",
     )(grads, local)
@@ -631,7 +655,7 @@
     head_queries, head_grads, pool = gather(queries, keys, values, out_grad, total_blocks)
     pool = pool.reshape(total_blocks, BLOCK, 2 * HD)
     query_grad, local_grads, all_grads = attend(
-        rand_blocks, rand_count, head_queries, head_grads, pool, direct=True
+        rand_blocks.T, rand_count, head_queries, head_grads, pool, direct=True
     )
     key_grad, value_grad = reduce(
         all_grads.reshape(total_blocks * BLOCK, 2 * HD), local_grads.reshape(SHARD, 2 * HD)

time: 116 us -> 113 us (0.974)
  Pallas kernels: 111 us -> 109 us
    pallas_call x1, Pallas kernels: 41.7 us -> 40.1 us  [reduce(): pl.pallas_call(reduce_kernel, in_specs=[pl.BlockSpec(memory_space=pl.ANY)...]
    unnamed x5 -> x2, local copies, waits for them, and re-layouts: 3.89 us -> 3.23 us
where the time goes in v4:
time: 113 us
  Pallas kernels  109 us (96%)
  local copies, waits for them, and re-layouts  3.23 us (3%)
    pallas_call x1, Pallas kernels, gather(): pl.pallas_call(gather_kernel, in_specs=[anywhere] * 4, out_specs=[anywher...  47 us
    pallas_call x1, Pallas kernels, reduce(): pl.pallas_call(reduce_kernel, in_specs=[pl.BlockSpec(memory_space=pl.ANY)...  40.1 us
    pallas_call x1, Pallas kernels, attend(): pl.pallas_call(functools.partial(attend_kernel, direct), grid_spec=pltpu....  21.6 us
    unnamed x2, local copies, waits for them, and re-layouts  3.23 us

profile of v4, /device:TPU:0, one launch (start us, length us, event | category | flops | bytes accessed | tf_op | source)
XLA Modules:
  0.0 112.6 jit_solution(9864019926898654413)
XLA Ops:
  0.6 47.0 %gather.1 = (bf16[768,512]{1,0:T(8,128)(2,1)}, bf16[768,512]{1,0:T(8,128)(2,1)}, bf16[12288,256]{1,0:T(8,128)(2,1)}) custom-call(bf16[384,1024]{1,0:T(8,128)(2,1)} %q_in.1, bf16[384,256]{1,0:T(8,128)(2,1)} %k_in.1, bf16[384,256]{1,0:T(8,128)(2,1)} %v_in.1, bf16[384,1024]{1,0:T(8,128)(2,1)} %g_in.1), custom_call_target="tpu_custom_call" | custom-call | tf_op jit(solution)/shard_map/gather/pallas_call | solution.py:436
  47.6 21.6 %attend.1 = (bf16[768,512]{1,0:T(8,128)(2,1)}, f32[6,128,256]{2,1,0:T(8,128)}, bf16[96,128,256]{2,1,0:T(8,128)(2,1)}) custom-call(s32[3,96]{1,0:T(4,128)} %bitcast.7, s32[96]{0:T(128)} %valid.1, bf16[768,512]{1,0:T(8,128)(2,1)} %get-tuple-element.11.query_ref, bf16[768,512]{1,0:T(8,128)(2,1)} %get-tuple-element.12.grad_ref, bf16[96,128,256]{2,1,0:T(8,128)(2,1)} %bitcast.5), custom_call_target="tpu_custom_call" | custom-call | tf_op jit(solution)/shard_map/attend/pallas_call | solution.py:111
  69.2 40.1 %reduce.1 = (bf16[768,128]{1,0:T(8,128)(2,1)}, bf16[768,128]{1,0:T(8,128)(2,1)}) custom-call(bf16[12288,256]{1,0:T(8,128)(2,1)} %bitcast.4, f32[768,256]{1,0:T(8,128)} %bitcast.6), custom_call_target="tpu_custom_call" | custom-call | tf_op jit(solution)/shard_map/reduce/pallas_call | solution.py:631
  109.4 1.6 %copy.11 = bf16[768,128]{1,0:T(8,128)(2,1)} copy(bf16[768,128]{1,0:T(8,128)(2,1)} %get-tuple-element.23) | data formatting | bytes 393216
  111.0 1.6 %copy.12 = bf16[768,128]{1,0:T(8,128)(2,1)} copy(bf16[768,128]{1,0:T(8,128)(2,1)} %get-tuple-element.24) | data formatting | bytes 393216
